TPU v7x, 128 devices: a whole 4x4x4 slice. The times are simulated.
128 devices in a mesh: ep: 64 (over y, z, x), tp: 2 (over core).
Axes of the slice: x: 4, y: 4, z: 4, core: 2. Of those that a mesh axis runs over, the one named last changes fastest.
Arguments:
- tokens: bfloat16 [8192, 3584], P('ep'), may hold values from -6 to 6
- expert_ids: int32 [8192, 8], P('ep'), may hold values from 0 to 63, all different within a row; in each aligned block of 128 rows (0 to 127, 128 to 255, ...) at most 24 rows name the same one
- gate_values: float32 [8192, 8], P('ep'), may hold values from 0.05 to 1
- w_gate: bfloat16 [64, 3584, 1024], P('ep', None, 'tp'), may hold values from -0.09375 to 0.09375
- w_up: bfloat16 [64, 3584, 1024], P('ep', None, 'tp'), may hold values from -0.09375 to 0.09375
- w_down: bfloat16 [64, 1024, 3584], P('ep', 'tp'), may hold values from -0.1875 to 0.1875
- shared_gate: bfloat16 [3584, 1024], P(None, 'tp'), may hold values from -0.09375 to 0.09375
- shared_up: bfloat16 [3584, 1024], P(None, 'tp'), may hold values from -0.09375 to 0.09375
- shared_down: bfloat16 [1024, 3584], P('tp'), may hold values from -0.1875 to 0.1875
Outputs:
- layer_out: bfloat16 [8192, 3584], P('ep', 'tp')
Inputs may be any that keep to these rules, and one draw needn't show every extreme that they name: `expert_ids`: each row names 8 different experts; within the rows of one index of ep (aligned blocks of 128 rows) no expert is named by more than 24 rows.
All inputs are finite; a program needn't handle non-finite values.
Results may differ from a plain program's by a relative error of at most 0.0085.
Values may be sent and summed in bfloat16 or wider, within the bound.
No kernel may reach another device: no remote copies, remote signals or barrier semaphores. Data moves between devices by JAX's collectives and lax.ppermute only.
A program may use at most 128 MiB of HBM per device.

v0:
```python
import jax
import jax.numpy as jnp
from jax import lax
from jax.sharding import PartitionSpec as P

route_scale = 2.827


def split_up(x, dim, count):
    dims = x.shape
    tiles = x.reshape(*dims[:dim], count, dims[dim] // count, *dims[dim + 1 :])
    return jnp.moveaxis(tiles, dim, 0)


def cut_rows(length, count):
    lap = length // count
    if lap >= 8:
        lap -= lap % 8
    return [lap * k for k in range(1, count)]


def in_order(tiles, dim):
    dims = list(tiles.shape[1:])
    dims[dim] *= tiles.shape[0]
    return jnp.moveaxis(tiles, 0, dim).reshape(dims)


def exchange_in_pieces(x, axis, pieces, split_dim, concat_dim):
    tiles = split_up(x, split_dim, lax.axis_size(axis))
    cut = max(range(1, max(2, tiles.ndim - 1)), key=lambda d: tiles.shape[d])
    outs = []
    for section in jnp.split(tiles, cut_rows(tiles.shape[cut], pieces), axis=cut):
        if section.size:
            outs.append(lax.all_to_all(section, axis, split_axis=0, concat_axis=0, tiled=True))
    return in_order(jnp.concatenate(outs, axis=cut), concat_dim)


def sum_at_owner(x, axis, dim):
    tiles = split_up(x, dim, lax.axis_size(axis))
    arrived = lax.all_to_all(tiles, axis, split_axis=0, concat_axis=0, tiled=True)
    return arrived.sum(axis=0)


def expert_apply(inputs, gate_matrix, up_matrix, down_matrix):
    gate_out = jnp.dot(inputs, gate_matrix, preferred_element_type=jnp.float32)
    up_out = jnp.dot(inputs, up_matrix, preferred_element_type=jnp.float32)
    hidden = (jax.nn.silu(gate_out) * up_out).astype(jnp.bfloat16)
    return jnp.dot(hidden, down_matrix, preferred_element_type=jnp.float32)


def combine_rows(returned, target, weights, tok_rows, top_count):
    feature_count = returned.shape[-1]
    picked = jnp.take(returned.reshape(-1, feature_count), target, axis=0)
    picked = picked.reshape(tok_rows, top_count, feature_count)
    return jnp.sum(picked * weights[:, :, None], axis=1)


def per_device(
    tokens, expert_ids, gate_values, w_gate, w_up, w_down, shared_gate, shared_up, shared_down
):
    ep_count = lax.axis_size("ep")
    tp_count = lax.axis_size("tp")
    tok_rows, model_width = tokens.shape
    top_count = expert_ids.shape[1]
    experts = ep_count * w_gate.shape[0]
    capacity = 3 * tok_rows * top_count // (2 * experts)
    weights = route_scale * gate_values / jnp.sum(gate_values, axis=1, keepdims=True)
    flat_ids = expert_ids.reshape(-1)
    onehot = (flat_ids[:, None] == jnp.arange(experts, dtype=jnp.int32)[None, :]).astype(jnp.int32)
    earlier = jnp.cumsum(onehot, axis=0) - onehot
    slot_index = jnp.sum(earlier * onehot, axis=1)
    target = flat_ids * capacity + slot_index
    row_owner = jnp.full((experts * capacity,), tok_rows, jnp.int32)
    row_owner = row_owner.at[target].set(
        jnp.arange(flat_ids.shape[0], dtype=jnp.int32) // top_count
    )
    half_width = model_width // tp_count
    source = lax.dynamic_slice_in_dim(tokens, lax.axis_index("tp") * half_width, half_width, 1)
    padded = jnp.concatenate([source, jnp.zeros((1, source.shape[1]), jnp.bfloat16)], axis=0)
    outgoing = jnp.take(padded, row_owner, axis=0).reshape(ep_count, capacity, source.shape[1])
    parted = lax.all_to_all(outgoing, "ep", split_axis=0, concat_axis=0, tiled=True)
    arrived = lax.all_gather(parted, "tp", axis=2, tiled=True)
    expert_rows = arrived.reshape(-1, model_width)
    partial_value = expert_apply(expert_rows, w_gate[0], w_up[0], w_down[0])
    shared = expert_apply(tokens, shared_gate, shared_up, shared_down)
    summed = lax.psum_scatter(
        partial_value.astype(jnp.bfloat16), "tp", scatter_dimension=1, tiled=True
    ).astype(jnp.float32)
    returned = exchange_in_pieces(
        summed.reshape(ep_count, capacity, summed.shape[1]).astype(jnp.bfloat16), "ep", 2, 0, 0
    ).astype(jnp.float32)
    routed = combine_rows(returned, target, weights, tok_rows, top_count)
    shared_own = sum_at_owner(shared, "tp", 1)
    return (routed + shared_own).astype(jnp.bfloat16)


def solution(mesh):
    return jax.shard_map(
        per_device,
        mesh=mesh,
        in_specs=(
            P("ep", None),
            P("ep", None),
            P("ep", None),
            P("ep", None, "tp"),
            P("ep", None, "tp"),
            P("ep", "tp", None),
            P(None, "tp"),
            P(None, "tp"),
            P("tp", None),
        ),
        out_specs=P("ep", "tp"),
        check_vma=False,
    )
```

profile of v0, /device:TPU:0, one launch (start us, length us, event | category | flops | bytes accessed | tf_op | source)
XLA Modules:
  0.0 325.0 jit_solution(9512787485436525865)
XLA Ops:
  6.5 0.9 copy.27
  7.6 0.7 broadcast_multiply_fusion
  8.3 18.0 %reduce-window.6 = s32[64,8,128]{2,1,0:T(8,128)S(1)} reduce-window(s32[64,8,128]{2,1,0:T(8,128)S(1)} %fusion.26, s32[]{:T(128)} %constant.40.clone.1), window={size=1x1x128 pad=0_0x0_0x127_0}, to_apply=%region_0.0 | reduce-window | flops 8323072 | bytes 524292 | tf_op jit(solution)/shard_map/reduce-window
  26.3 0.1 slice.12
  26.5 0.1 copy.29
  26.7 0.1 broadcast_add_fusion
  26.9 0.1 copy.33
  27.2 4.3 %scatter_custom_fusion = s32[1536]{0:T(1024)S(1)} fusion(s32[1024]{0:T(1024)S(1)} %bitcast.72, s32[1024]{0:T(1024)S(1)} %add_select_fusion, s32[]{:T(128)} %constant.62.clone.1), kind=kCustom, calls=%fused_computation.49 | custom fusion | bytes 6148 | tf_op jit(solution)/shard_map/scatter | solution.py:74
  31.7 6.7 %gather_fusion = bf16[1536,1792]{1,0:T(8,128)(2,1)} fusion(bf16[129,1792]{1,0:T(8,128)(2,1)S(1)} %concatenate.6, s32[2048]{0:T(1024)S(1)} %pad_clamp_fusion), kind=kCustom, calls=%fused_computation | custom fusion | bytes 11016192 | tf_op jit(solution)/shard_map/jit(_take)/gather | solution.py:80
  38.4 3.1 broadcast_select_fusion
  41.6 78.1 %all_to_all.20 = bf16[64,24,1792]{2,1,0:T(8,128)(2,1)} all-to-all(bf16[64,24,1792]{2,1,0:T(8,128)(2,1)S(1)} %broadcast_select_fusion), channel_id=1, replica_groups=mesh['ep'=64,'tp'=2] {'ep'}, dimensions={0} | all-to-all | bytes 11010048 | tf_op jit(solution)/shard_map/all_to_all | solution.py:81
  119.8 22.8 %all-gather.2.cloned.1.call-done = bf16[64,24,3584]{2,1,0:T(8,128)(2,1)} async-done(((bf16[64,24,1792]{2,1,0:T(8,128)(2,1)}), bf16[64,24,3584]{2,1,0:T(8,128)(2,1)}) %all-gather.2.cloned.1.call-update) | async-done | bytes 11010064 | tf_op jit(solution)/shard_map/all_gather | solution.py:82
  142.5 10.8 %fusion.5 = f32[1536,512]{1,0:T(8,128)} fusion(bf16[1536,3584]{1,0:T(8,128)(2,1)} %bitcast.74, bf16[1,3584,512]{2,1,0:T(8,128)(2,1)} %param.12), kind=kOutput, calls=%fused_computation.13 | convolution fusion | flops 5637144576 | bytes 17825792 | tf_op jit(solution)/shard_map/dot_general | solution.py:45
  153.4 19.5 %convolution_convert_fusion = bf16[1536,3584]{1,0:T(8,128)(2,1)} fusion(bf16[1,512,3584]{2,1,0:T(8,128)(2,1)} %param.14, bf16[1536,3584]{1,0:T(8,128)(2,1)} %bitcast.75, bf16[1,3584,512]{2,1,0:T(8,128)(2,1)} %param.13, f32[1536,512]{1,0:T(8,128)} %fusion.5), kind=kOutput, calls=%fused_computation.3 | convolution fusion | flops 11284512768 | bytes 32505856 | tf_op jit(solution)/shard_map/dot_general | solution.py:48
  172.9 2.7 fusion.35
  175.5 4.4 %fusion.17 = f32[128,3584]{1,0:T(8,128)S(1)} fusion(bf16[512,3584]{1,0:T(8,128)(2,1)} %param.17, bf16[128,3584]{1,0:T(8,128)(2,1)S(1)} %copy-done, bf16[3584,512]{1,0:T(8,128)(2,1)} %param.16, f32[128,512]{1,0:T(8,128)S(1)} %fusion.35), kind=kOutput, calls=%fused_computation.21 | convolution fusion | flops 939917312 | bytes 10354688 | tf_op jit(solution)/shard_map/dot_general | solution.py:48
  179.9 1.4 copy.42
  181.3 3.8 %all-to-all-start.3 = ((f32[2,128,1792]{2,1,0:T(8,128)}), f32[2,128,1792]{2,1,0:T(8,128)S(1)}, u32[]{:S(2)}, u32[]{:S(2)}) async-start(f32[2,128,1792]{2,1,0:T(8,128)} %bitcast.66), calls=%async_computation.4 | async-start | bytes 3670016 | tf_op jit(solution)/shard_map/all_to_all | solution.py:40
  185.1 11.0 %reduce-scatter.2.cloned.1.call-done = bf16[1536,1792]{1,0:T(8,128)(2,1)} async-done(((bf16[1536,3584]{1,0:T(8,128)(2,1)}), bf16[1536,1792]{1,0:T(8,128)(2,1)}) %reduce-scatter.2.cloned.1.call-update) | async-done | bytes 5505040 | tf_op jit(solution)/shard_map/reduce_scatter | solution.py:86
  196.1 2.9 split.8
  198.9 10.6 %all-to-all-start.1 = ((bf16[64,1,8,1792]{3,2,1,0:T(8,128)(2,1)}), bf16[64,1,8,1792]{3,2,1,0:T(8,128)(2,1)}, u32[]{:S(2)}, u32[]{:S(2)}) async-start(bf16[64,1,8,1792]{3,2,1,0:T(8,128)(2,1)} %split.8), calls=%async_computation.2 | async-start | bytes 3670016 | tf_op jit(solution)/shard_map/all_to_all | solution.py:34
  209.5 4.1 %split.9 = bf16[64,1,16,1792]{3,2,1,0:T(8,128)(2,1)} slice(bf16[64,1,24,1792]{3,2,1,0:T(8,128)(2,1)} %bitcast.68), slice={[0:64], [0:1], [8:24], [0:1792]} | slice | bytes 7340032 | tf_op jit(solution)/shard_map/split | solution.py:32
  213.6 24.1 %all-to-all-done.1 = bf16[64,1,8,1792]{3,2,1,0:T(8,128)(2,1)} async-done(((bf16[64,1,8,1792]{3,2,1,0:T(8,128)(2,1)}), bf16[64,1,8,1792]{3,2,1,0:T(8,128)(2,1)}, u32[]{:S(2)}, u32[]{:S(2)}) %all-to-all-start.1) | async-done | bytes 1835040 | tf_op jit(solution)/shard_map/all_to_all | solution.py:34
  237.7 5.6 %all-to-all-start.2 = ((bf16[64,1,16,1792]{3,2,1,0:T(8,128)(2,1)}), bf16[64,1,16,1792]{3,2,1,0:T(8,128)(2,1)}, u32[]{:S(2)}, u32[]{:S(2)}) async-start(bf16[64,1,16,1792]{3,2,1,0:T(8,128)(2,1)} %split.9), calls=%async_computation.3 | async-start | bytes 7340032 | tf_op jit(solution)/shard_map/all_to_all | solution.py:34
  243.5 0.1 copy.32
  243.8 1.1 reduce_sum.45
  244.9 46.4 %all-to-all-done.2 = bf16[64,1,16,1792]{3,2,1,0:T(8,128)(2,1)} async-done(((bf16[64,1,16,1792]{3,2,1,0:T(8,128)(2,1)}), bf16[64,1,16,1792]{3,2,1,0:T(8,128)(2,1)}, u32[]{:S(2)}, u32[]{:S(2)}) %all-to-all-start.2) | async-done | bytes 3670048 | tf_op jit(solution)/shard_map/all_to_all | solution.py:34
  291.3 3.0 pad_maximum_fusion
  294.3 5.4 %bitcast_convert_fusion = f32[1536,1792]{1,0:T(8,128)} fusion(bf16[64,1,24,1792]{3,2,1,0:T(8,128)(2,1)S(1)} %pad_maximum_fusion), kind=kLoop, calls=%fused_computation.8 | loop fusion | flops 2752512 | bytes 16515072 | tf_op jit(solution)/shard_map/convert_element_type | solution.py:91
  299.7 12.4 %gather_fusion.1 = f32[1024,1792]{1,0:T(8,128)} fusion(f32[1536,1792]{1,0:T(8,128)} %bitcast_convert_fusion, s32[1024]{0:T(1024)S(1)} %broadcast_clamp_fusion), kind=kCustom, calls=%fused_computation.1 | custom fusion | bytes 14684160 | tf_op jit(solution)/shard_map/jit(_take)/gather | solution.py:53
  312.1 5.2 %fusion.1 = f32[128,1792]{1,0:T(8,128)S(1)} fusion(f32[1024,1792]{1,0:T(8,128)} %gather_fusion.1, f32[128,8]{1,0:T(8,128)S(1)} %copy.36, pred[128,8]{1,0:T(8,128)(4,1)S(1)} %copy.32), kind=kLoop, calls=%fused_computation.6 | loop fusion | flops 5275648 | bytes 8262656 | tf_op jit(solution)/shard_map/reduce_sum | solution.py:55
  317.3 0.9 add_convert_fusion
  (36 shorter events, 1.1 us)
Async XLA Ops:
  6.5 25.1 %copy-start = (bf16[128,3584]{1,0:T(8,128)(2,1)S(1)}, bf16[128,3584]{1,0:T(8,128)(2,1)}, u32[]{:S(2)}) copy-start(bf16[128,3584]{1,0:T(8,128)(2,1)} %param.9) | copy-start | bytes 2752516
  6.5 136.0 %all-gather.2.cloned.1.call-start = ((), (), s32[]{:S(2)}) async-start(), calls=%async_computation.5 | async-start | bytes 16515072 | tf_op jit(solution)/shard_map/all_gather | solution.py:82
  119.7 76.4 %reduce-scatter.2.cloned.1.call-start = ((), (), s32[]{:S(2)}) async-start(), calls=%async_computation.6 | async-start | bytes 16515072 | tf_op jit(solution)/shard_map/reduce_scatter | solution.py:86
  181.3 17.6 %all-to-all-start.3 = ((f32[2,128,1792]{2,1,0:T(8,128)}), f32[2,128,1792]{2,1,0:T(8,128)S(1)}, u32[]{:S(2)}, u32[]{:S(2)}) async-start(f32[2,128,1792]{2,1,0:T(8,128)} %bitcast.66), calls=%async_computation.4 | async-start | bytes 3670016 | tf_op jit(solution)/shard_map/all_to_all | solution.py:40
  198.9 38.8 %all-to-all-start.1 = ((bf16[64,1,8,1792]{3,2,1,0:T(8,128)(2,1)}), bf16[64,1,8,1792]{3,2,1,0:T(8,128)(2,1)}, u32[]{:S(2)}, u32[]{:S(2)}) async-start(bf16[64,1,8,1792]{3,2,1,0:T(8,128)(2,1)} %split.8), calls=%async_computation.2 | async-start | bytes 3670016 | tf_op jit(solution)/shard_map/all_to_all | solution.py:34
  213.6 29.9 %copy-start.2 = (s32[128,8]{0,1:T(8,128)S(1)}, s32[128,8]{0,1:T(8,128)}, u32[]{:S(2)}) copy-start(s32[128,8]{0,1:T(8,128)} %param.10) | copy-start | bytes 12292
  213.6 30.0 %copy-start.3 = (f32[128,8]{0,1:T(8,128)S(1)}, f32[128,8]{0,1:T(8,128)}, u32[]{:S(2)}) copy-start(f32[128,8]{0,1:T(8,128)} %param.11) | copy-start | bytes 12292
  237.7 53.6 %all-to-all-start.2 = ((bf16[64,1,16,1792]{3,2,1,0:T(8,128)(2,1)}), bf16[64,1,16,1792]{3,2,1,0:T(8,128)(2,1)}, u32[]{:S(2)}, u32[]{:S(2)}) async-start(bf16[64,1,16,1792]{3,2,1,0:T(8,128)(2,1)} %split.9), calls=%async_computation.3 | async-start | bytes 7340032 | tf_op jit(solution)/shard_map/all_to_all | solution.py:34
  312.1 5.2 %copy-start.1 = (f32[128,1792]{1,0:T(8,128)S(1)}, f32[128,1792]{1,0:T(8,128)}, u32[]{:S(2)}) copy-start(f32[128,1792]{1,0:T(8,128)} %reduce_sum.45) | copy-start | bytes 2752516
Sparse Core Ops, SparseCore 0:
  119.8 22.6 all-gather.1
  173.0 23.0 reduce-scatter.1
where the time goes:
time: 326 us; the launch traced here: 325 us
  waiting for transfers between devices  104 us (32%)
  blocking collectives  78.1 us (24%)
  other arithmetic  37.6 us (12%)
  matrix products  37.4 us (11%)
  local copies, waits for them, and re-layouts  33.9 us (10%)
  starting transfers between devices  20 us (6%)
  between operations  13.6 us (4%)
    all_to_all x1, blocking collectives, per_device(): lax.all_to_all(outgoing, 'ep', split_axis=0, concat_axis=0, tiled=True)  78.1 us
    all_to_all x2, waiting for transfers between devices, exchange_in_pieces(): lax.all_to_all(section, axis, split_axis=0, concat_axis=0, tiled=True)  70.5 us
    dot_general x2, matrix products, expert_apply(): return jnp.dot(hidden, down_matrix, preferred_element_type=jnp.float32)  23.9 us
    all_gather x1, waiting for transfers between devices, per_device(): arrived = lax.all_gather(parted, 'tp', axis=2, tiled=True)  22.8 us
    another operation x3, other arithmetic  18.2 us
    all_to_all x2, starting transfers between devices, exchange_in_pieces(): lax.all_to_all(section, axis, split_axis=0, concat_axis=0, tiled=True)  16.2 us
    dot_general x2, matrix products, expert_apply(): gate_out = jnp.dot(inputs, gate_matrix, preferred_element_type=jnp.float32)  13.5 us
    gather x1, local copies, waits for them, and re-layouts, combine_rows(): picked = jnp.take(returned.reshape(-1, feature_count), target, axis=0)  12.4 us
  transfers between devices with their start and end apart: 5, of which 4 were waited for; matrix products, arithmetic and copies ran while one was open for 5% of the time, Pallas kernels for 0%

commit v1 on v0

v1 whole, which is shorter than its diff:
```python
import functools

import jax
import jax.numpy as jnp
from jax import lax
from jax.experimental import pallas as pl
from jax.experimental.pallas import tpu as pltpu
from jax.sharding import PartitionSpec as P


route_scale = 2.827
TILE = 8
F32 = jnp.float32
BF16 = jnp.bfloat16
NT = (((1,), (1,)), ((), ()))


def named(ids, experts):
    rows, top = ids.shape
    column = lax.broadcasted_iota(jnp.int32, (rows, experts), 1)
    return column, [(ids[:, k : k + 1] == column).astype(F32) for k in range(top)]


def ranks(ids, experts):
    rows = ids.shape[0]
    _, hits = named(ids, experts)
    chosen = functools.reduce(jnp.add, hits)
    row = lax.broadcasted_iota(jnp.int32, (rows, rows), 0)
    col = lax.broadcasted_iota(jnp.int32, (rows, rows), 1)
    before = (col < row).astype(F32).astype(BF16)
    rank = jnp.dot(before, chosen.astype(BF16), preferred_element_type=F32)
    return jnp.where(chosen > 0, rank, -1.0), hits


def pick_rows(ids, experts, first):
    rank, _ = ranks(ids, experts)
    count = experts * TILE
    slot = lax.broadcasted_iota(jnp.int32, (count, experts), 0)
    expert = lax.broadcasted_iota(jnp.int32, (count, experts), 1)
    spread = (lax.shift_right_logical(slot, 3) == expert).astype(F32).astype(BF16)
    wide = lax.dot_general(spread, rank.astype(BF16), NT, preferred_element_type=F32)
    place = lax.broadcasted_iota(jnp.int32, wide.shape, 0) & (TILE - 1)
    return (wide == (place + first).astype(F32)).astype(F32).astype(BF16)


def weigh_rows(ids, gates, experts, first):
    rank, hits = ranks(ids, experts)
    weights = route_scale * gates / jnp.sum(gates, axis=1, keepdims=True)
    by_expert = functools.reduce(
        jnp.add, [hit * weights[:, k : k + 1] for k, hit in enumerate(hits)]
    )
    count = experts * TILE
    expert = lax.broadcasted_iota(jnp.int32, (experts, count), 0)
    slot = lax.broadcasted_iota(jnp.int32, (experts, count), 1)
    spread = (lax.shift_right_logical(slot, 3) == expert).astype(F32).astype(BF16)
    wide = jnp.dot(rank.astype(BF16), spread, preferred_element_type=F32)
    place = lax.broadcasted_iota(jnp.int32, wide.shape, 1) & (TILE - 1)
    here = wide == (place + first).astype(F32)
    high = by_expert.astype(BF16)
    low = (by_expert - high.astype(F32)).astype(BF16)
    parts = [
        jnp.where(here, jnp.dot(part, spread, preferred_element_type=F32), 0.0).astype(BF16)
        for part in (high, low)
    ]
    return jnp.concatenate(parts, axis=0)


def dispatch_body(experts, tail, core, ids, tokens, out, picks):
    @pl.when(pl.program_id(0) == 0)
    def _():
        first = 2 * TILE if tail else core[0] * TILE
        picks[...] = pick_rows(ids[...], experts, first)

    out[...] = jnp.dot(picks[...], tokens[...], preferred_element_type=F32).astype(BF16)


def dispatch(core, ids, tokens, experts, tail):
    rows, width = tokens.shape
    block = width // 4
    steps = 2 if tail else 4
    column = (lambda i, c: (0, 2 * c[0] + i)) if tail else (lambda i, c: (0, i))
    return pl.pallas_call(
        functools.partial(dispatch_body, experts, tail),
        out_shape=jax.ShapeDtypeStruct((experts * TILE, steps * block), BF16),
        grid_spec=pltpu.PrefetchScalarGridSpec(
            num_scalar_prefetch=1,
            grid=(steps,),
            in_specs=[
                pl.BlockSpec(ids.shape, lambda i, c: (0, 0)),
                pl.BlockSpec((rows, block), column),
            ],
            out_specs=pl.BlockSpec((experts * TILE, block), lambda i, c: (0, i)),
            scratch_shapes=[pltpu.VMEM((experts * TILE, rows), BF16)],
        ),
        name="dispatch_tail" if tail else "dispatch_head",
    )(core, ids, tokens)


def tables_body(experts, core, ids, gates, head, tail):
    head[...] = weigh_rows(ids[...], gates[...], experts, core[0] * TILE)
    tail[...] = weigh_rows(ids[...], gates[...], experts, 2 * TILE)


def tables(core, ids, gates, experts):
    shape = jax.ShapeDtypeStruct((2 * ids.shape[0], experts * TILE), BF16)
    whole = lambda s: pl.BlockSpec(s, lambda i, c: (0, 0))
    return pl.pallas_call(
        functools.partial(tables_body, experts),
        out_shape=(shape, shape),
        grid_spec=pltpu.PrefetchScalarGridSpec(
            num_scalar_prefetch=1,
            grid=(1,),
            in_specs=[whole(ids.shape), whole(gates.shape)],
            out_specs=(whole(shape.shape), whole(shape.shape)),
        ),
        name="weight_tables",
    )(core, ids, gates)


def expert_steps(core, steps, xs, own, other, total):
    step = pl.program_id(0)

    def add(g, u, d):
        gate_out = up_out = None
        for p, x in enumerate(xs):
            width = x.shape[1]
            where = p + core - 2 * p * core
            span = slice(None) if len(xs) == 1 else pl.ds(pl.multiple_of(where * width, 128), width)
            a = jnp.dot(x[...], g[span, :], preferred_element_type=F32)
            b = jnp.dot(x[...], u[span, :], preferred_element_type=F32)
            gate_out = a if gate_out is None else gate_out + a
            up_out = b if up_out is None else up_out + b
        hidden = (gate_out / (1.0 + jnp.exp(-gate_out)) * up_out).astype(BF16)
        return jnp.dot(hidden, d[...], preferred_element_type=F32)

    @pl.when(step == 0)
    def _():
        total[...] = add(*own)

    @pl.when((step > 0) & (step < steps))
    def _():
        total[...] += add(*own)

    @pl.when(step >= steps)
    def _():
        total[...] += add(*other)

    return step == 2 * steps - 1


def head_body(steps, core, x, g0, u0, d0, g1, u1, d1, out, total):
    last = expert_steps(core[0], steps, (x,), (g0, u0, d0), (g1, u1, d1), total)

    @pl.when(last)
    def _():
        out[...] = total[...].astype(BF16)


def tail_body(steps, core, x0, x1, g0, u0, d0, g1, u1, d1, keep, send, total):
    last = expert_steps(core[0], steps, (x0, x1), (g0, u0, d0), (g1, u1, d1), total)

    @pl.when(last)
    def _():
        width = keep.shape[1]
        mine = pl.multiple_of(core[0] * width, 128)
        theirs = pl.multiple_of((1 - core[0]) * width, 128)
        keep[...] = total[:, pl.ds(mine, width)].astype(BF16)
        send[...] = total[:, pl.ds(theirs, width)].astype(BF16)


def expert_apply(core, xs, own, other):
    rows = xs[0].shape[-2]
    width, hidden = own[0].shape
    block = 256
    steps = hidden // block
    first = lambda i: jnp.minimum(i, steps - 1)
    second = lambda i: jnp.maximum(i - steps, 0)
    specs = []
    for pick in (first, second):
        specs += [pl.BlockSpec((width, block), lambda i, c, pick=pick: (0, pick(i)))] * 2
        specs += [pl.BlockSpec((block, width), lambda i, c, pick=pick: (pick(i), 0))]
    once = pl.Buffered(1)
    whole = lambda s: pl.BlockSpec(s, lambda i, c: (0, 0), pipeline_mode=once)
    if len(xs) == 1:
        x_specs = [whole(xs[0].shape)]
        out = jax.ShapeDtypeStruct((rows, width), BF16)
        body, out_specs = head_body, whole(out.shape)
    else:
        half = width // 2
        mine = pl.BlockSpec((pl.Squeezed(), rows, half), lambda i, c: (c[0], 0, 0), pipeline_mode=once)
        x_specs = [mine, whole((rows, half))]
        out = (jax.ShapeDtypeStruct((rows, half), BF16),) * 2
        body, out_specs = tail_body, (whole((rows, half)),) * 2
    return pl.pallas_call(
        functools.partial(body, steps),
        out_shape=out,
        grid_spec=pltpu.PrefetchScalarGridSpec(
            num_scalar_prefetch=1,
            grid=(2 * steps,),
            in_specs=x_specs + specs,
            out_specs=out_specs,
            scratch_shapes=[pltpu.VMEM((rows, width), F32)],
        ),
        cost_estimate=pl.CostEstimate(
            flops=12 * rows * width * hidden,
            transcendentals=2 * rows * hidden,
            bytes_accessed=4 * rows * width + 12 * width * hidden,
        ),
        compiler_params=pltpu.CompilerParams(vmem_limit_bytes=56 << 20),
    )(core, *xs, *own, *other)


def weighted(table, rows):
    both = jnp.dot(table, rows, preferred_element_type=F32)
    half = both.shape[0] // 2
    return both[:half] + both[half:]


def combine_head_body(core, table, rows, shared, send, keep):
    value = weighted(table[...], rows[...]) + shared[...]

    @pl.when(pl.program_id(0) < 2)
    def _():
        send[...] = value

    @pl.when(pl.program_id(0) >= 2)
    def _():
        keep[...] = value


def combine_head(core, table, rows, shared):
    count, width = rows.shape
    tokens = shared.shape[0]
    block = width // 4
    column = lambda i, c: (0, jnp.where(i < 2, 2 * (1 - c[0]) + i, 2 * c[0] + i - 2))
    out = jax.ShapeDtypeStruct((tokens, 2 * block), F32)
    return pl.pallas_call(
        combine_head_body,
        out_shape=(out, out),
        grid_spec=pltpu.PrefetchScalarGridSpec(
            num_scalar_prefetch=1,
            grid=(4,),
            in_specs=[
                pl.BlockSpec(table.shape, lambda i, c: (0, 0)),
                pl.BlockSpec((count, block), column),
                pl.BlockSpec((tokens, block), column),
            ],
            out_specs=(
                pl.BlockSpec((tokens, block), lambda i, c: (0, jnp.minimum(i, 1))),
                pl.BlockSpec((tokens, block), lambda i, c: (0, jnp.maximum(i - 2, 0))),
            ),
        ),
        name="combine_head",
    )(core, table, rows, shared)


def combine_tail_body(table, rows, keep, received, out):
    value = weighted(table[...], rows[...]) + (keep[...] + received[...])
    out[...] = value.astype(BF16)


def combine_tail(table, rows, keep, received):
    count, width = rows.shape
    tokens = keep.shape[0]
    block = width // 2
    return pl.pallas_call(
        combine_tail_body,
        out_shape=jax.ShapeDtypeStruct((tokens, width), BF16),
        grid=(2,),
        in_specs=[
            pl.BlockSpec(table.shape, lambda i: (0, 0)),
            pl.BlockSpec((count, block), lambda i: (0, i)),
            pl.BlockSpec((tokens, block), lambda i: (0, i)),
            pl.BlockSpec((tokens, block), lambda i: (0, i)),
        ],
        out_specs=pl.BlockSpec((tokens, block), lambda i: (0, i)),
        name="combine_tail",
    )(table, rows, keep, received)


def shared_apply(inputs, gate_matrix, up_matrix, down_matrix):
    gate_out = jnp.dot(inputs, gate_matrix, preferred_element_type=F32)
    up_out = jnp.dot(inputs, up_matrix, preferred_element_type=F32)
    hidden = (jax.nn.silu(gate_out) * up_out).astype(BF16)
    return jnp.dot(hidden, down_matrix, preferred_element_type=F32)


def exchange(x, axis):
    return lax.all_to_all(x, axis, split_axis=0, concat_axis=0, tiled=True)


def per_device(
    tokens, expert_ids, gate_values, w_gate, w_up, w_down, shared_gate, shared_up, shared_down
):
    experts = lax.axis_size("ep") * w_gate.shape[0]
    width = tokens.shape[1]
    half = width // 2
    core = lax.axis_index("tp").astype(jnp.int32).reshape(1)
    swap = [(0, 1), (1, 0)]
    own = (w_gate[0], w_up[0], w_down[0])
    other = tuple(lax.ppermute(w, "tp", swap) for w in own)
    head = dispatch(core, expert_ids, tokens, experts, False)
    head_in = exchange(head.reshape(experts, TILE, width), "ep")
    tail = dispatch(core, expert_ids, tokens, experts, True)
    tail_in = exchange(tail.reshape(experts, TILE, half), "ep")
    table_head, table_tail = tables(core, expert_ids, gate_values, experts)
    shared = shared_apply(tokens, shared_gate, shared_up, shared_down)
    head_out = expert_apply(core, (head_in.reshape(experts * TILE, width),), own, other)
    head_back = exchange(head_out.reshape(experts, TILE, width), "ep")
    tail_x = tail_in.reshape(2, experts * TILE // 2, half)
    theirs = lax.dynamic_index_in_dim(tail_x, 1 - core[0], 0, keepdims=False)
    theirs = lax.ppermute(theirs, "tp", swap)
    kept, sent = expert_apply(core, (tail_x, theirs), own, other)
    taken = lax.ppermute(sent, "tp", swap)
    tail_y = jnp.where(core[0] == 0, jnp.stack([kept, taken]), jnp.stack([taken, kept]))
    tail_back = exchange(tail_y.reshape(experts, TILE, half), "ep")
    send, keep = combine_head(core, table_head, head_back.reshape(-1, width), shared)
    received = lax.ppermute(send, "tp", swap)
    return combine_tail(table_tail, tail_back.reshape(-1, half), keep, received)


def solution(mesh):
    return jax.shard_map(
        per_device,
        mesh=mesh,
        in_specs=(
            P("ep", None),
            P("ep", None),
            P("ep", None),
            P("ep", None, "tp"),
            P("ep", None, "tp"),
            P("ep", "tp", None),
            P(None, "tp"),
            P(None, "tp"),
            P("tp", None),
        ),
        out_specs=P("ep", "tp"),
        check_vma=False,
    )
```

time: 326 us -> 187 us (0.57)
  blocking collectives: 78.1 us -> 0 us
  Pallas kernels: 0 us -> 54.7 us
  other arithmetic: 37.6 us -> 3.12 us
  local copies, waits for them, and re-layouts: 33.9 us -> 4.73 us
  matrix products: 37.4 us -> 8.34 us
  waiting for transfers between devices: 104 us -> 86.4 us
  between operations: 13.6 us -> 0.12 us
  starting transfers between devices: 20 us -> 28.6 us
    all_to_all x1 -> x0, blocking collectives: 78.1 us -> none  [per_device(): lax.all_to_all(outgoing, 'ep', split_axis=0, concat_axis=0, tiled=True)]
    pallas_call x0 -> x7, Pallas kernels: none -> 54.7 us  [the longest x2 34.8 us: expert_apply(): pl.pallas_call(functools.partial(body, steps), out_shape=out, grid_spec=p...]
    dot_general x4 -> x2, matrix products: 37.4 us -> 8.34 us  [the longest x1 5.66 us: shared_apply(): return jnp.dot(hidden, down_matrix, preferred_element_type=F32)]
    all_gather x1 -> x0, waiting for transfers between devices: 22.8 us -> none  [per_device(): arrived = lax.all_gather(parted, 'tp', axis=2, tiled=True)]
    gather x2 -> x0, local copies, waits for them, and re-layouts: 19.1 us -> none  [the longest x1 12.4 us: combine_rows(): picked = jnp.take(returned.reshape(-1, feature_count), target, axis=0)]
    another operation x3 -> x0, other arithmetic: 18.2 us -> none
    reduce_scatter x1 -> x0, waiting for transfers between devices: 11 us -> none  [per_device(): lax.psum_scatter(partial_value.astype(jnp.bfloat16), 'tp', scatter_dimens...]
    all_to_all x3 -> x4, waiting for transfers between devices: 70.6 us -> 81.4 us  [exchange(): return lax.all_to_all(x, axis, split_axis=0, concat_axis=0, tiled=True)]
  transfers between devices with their start and end apart: 5 -> 10, of which waited for: 4 -> 6; matrix products, arithmetic and copies ran while one was open for 5% -> 7% of each run, Pallas kernels for 0% -> 25%
where the time goes in v1:
time: 187 us; the launch traced here: 186 us
  waiting for transfers between devices  86.4 us (46%)
  Pallas kernels  54.7 us (29%)
  starting transfers between devices  28.6 us (15%)
  matrix products  8.34 us (4%)
  local copies, waits for them, and re-layouts  4.73 us (3%)
  other arithmetic  3.12 us (2%)
    all_to_all x4, waiting for transfers between devices, exchange(): return lax.all_to_all(x, axis, split_axis=0, concat_axis=0, tiled=True)  81.4 us
    pallas_call x2, Pallas kernels, expert_apply(): pl.pallas_call(functools.partial(body, steps), out_shape=out, grid_spec=p...  34.8 us
    all_to_all x4, starting transfers between devices, exchange(): return lax.all_to_all(x, axis, split_axis=0, concat_axis=0, tiled=True)  27.7 us
    pallas_call x2, Pallas kernels, dispatch(): pl.pallas_call(functools.partial(dispatch_body, experts, tail), out_shape...  8.52 us
    dot_general x1, matrix products, shared_apply(): return jnp.dot(hidden, down_matrix, preferred_element_type=F32)  5.66 us
    pallas_call x1, Pallas kernels, combine_head(): pl.pallas_call(combine_head_body, out_shape=(out, out), grid_spec=pltpu.P...  5.44 us
    unnamed x14, local copies, waits for them, and re-layouts  4.66 us
  transfers between devices with their start and end apart: 10, of which 6 were waited for; matrix products, arithmetic and copies ran while one was open for 7% of the time, Pallas kernels for 25%

profile of v1, /device:TPU:0, one launch (start us, length us, event | category | flops | bytes accessed | tf_op | source)
XLA Modules:
  0.0 186.0 jit_solution(5667898255345835167)
XLA Ops:
  0.0 1.4 copy.10.ids
  1.4 5.2 %dispatch_head.1 = bf16[512,3584]{1,0:T(8,128)(2,1)} custom-call(s32[1]{0:T(128)} %bitcast.core, s32[128,8]{1,0:T(8,128)} %copy.10.ids, bf16[128,3584]{1,0:T(8,128)(2,1)} %tokens.3), custom_call_target="tpu_custom_call" | custom-call | tf_op jit(solution)/shard_map/dispatch_head/pallas_call | solution.py:82
  6.6 11.8 %all-to-all-start.2 = ((bf16[64,8,3584]{2,1,0:T(8,128)(2,1)}), bf16[64,8,3584]{2,1,0:T(8,128)(2,1)}, u32[]{:S(2)}, u32[]{:S(2)}) async-start(bf16[64,8,3584]{2,1,0:T(8,128)(2,1)} %bitcast.21), calls=%async_computation.2 | async-start | bytes 7340032 | tf_op jit(solution)/shard_map/all_to_all | solution.py:289
  18.4 0.1 collective-permute-start.1
  18.5 0.5 collective-permute-start.2
  19.0 0.1 collective-permute-start.3
  19.1 3.3 %dispatch_tail.1 = bf16[512,1792]{1,0:T(8,128)(2,1)} custom-call(s32[1]{0:T(128)} %bitcast.core, s32[128,8]{1,0:T(8,128)} %copy.10.ids, bf16[128,3584]{1,0:T(8,128)(2,1)} %tokens.3), custom_call_target="tpu_custom_call" | custom-call | tf_op jit(solution)/shard_map/dispatch_tail/pallas_call | solution.py:82
  22.4 44.3 %all-to-all-done.2 = bf16[64,8,3584]{2,1,0:T(8,128)(2,1)} async-done(((bf16[64,8,3584]{2,1,0:T(8,128)(2,1)}), bf16[64,8,3584]{2,1,0:T(8,128)(2,1)}, u32[]{:S(2)}, u32[]{:S(2)}) %all-to-all-start.2) | async-done | bytes 3670048 | tf_op jit(solution)/shard_map/all_to_all | solution.py:289
  66.7 5.2 %all-to-all-start = ((bf16[64,8,1792]{2,1,0:T(8,128)(2,1)}), bf16[64,8,1792]{2,1,0:T(8,128)(2,1)S(1)}, u32[]{:S(2)}, u32[]{:S(2)}) async-start(bf16[64,8,1792]{2,1,0:T(8,128)(2,1)} %bitcast.26), calls=%async_computation | async-start | bytes 3670016 | tf_op jit(solution)/shard_map/all_to_all | solution.py:289
  71.9 0.0 collective-permute-done.3.d1
  71.9 20.3 %shard_map.92 = bf16[512,3584]{1,0:T(8,128)(2,1)} custom-call(s32[1]{0:T(128)} %bitcast.core, bf16[512,3584]{1,0:T(8,128)(2,1)} %bitcast.12.x, bf16[3584,512]{1,0:T(8,128)(2,1)} %bitcast.29, bf16[3584,512]{1,0:T(8,128)(2,1)} %bitcast.32, bf16[512,3584]{1,0:T(8,128)(2,1)} %bitcast.35, bf16[3584,512]{1,0:T(8,128)(2,1)} %collective-permute-done.1.g1, ...), custom_call_target="tpu_custom_call" | custom-call | flops 11274289152 | bytes 29360128 | tf_op jit(solution)/shard_map/pallas_call | solution.py:194
  92.3 6.3 %all-to-all-done = bf16[64,8,1792]{2,1,0:T(8,128)(2,1)S(1)} async-done(((bf16[64,8,1792]{2,1,0:T(8,128)(2,1)}), bf16[64,8,1792]{2,1,0:T(8,128)(2,1)S(1)}, u32[]{:S(2)}, u32[]{:S(2)}) %all-to-all-start) | async-done | bytes 1835040 | tf_op jit(solution)/shard_map/all_to_all | solution.py:289
  98.6 5.8 %all-to-all-start.3 = ((bf16[64,8,3584]{2,1,0:T(8,128)(2,1)}), bf16[64,8,3584]{2,1,0:T(8,128)(2,1)}, u32[]{:S(2)}, u32[]{:S(2)}) async-start(bf16[64,8,3584]{2,1,0:T(8,128)(2,1)} %bitcast.27), calls=%async_computation.3 | async-start | bytes 7340032 | tf_op jit(solution)/shard_map/all_to_all | solution.py:289
  104.4 0.1 dynamic-slice_bitcast_fusion
  104.5 0.1 collective-permute-start
  104.6 2.5 %collective-permute-done.x1 = bf16[256,1792]{1,0:T(8,128)(2,1)S(1)} collective-permute-done((bf16[256,1792]{1,0:T(8,128)(2,1)S(1)}, bf16[256,1792]{1,0:T(8,128)(2,1)S(1)}, u32[]{:S(2)}, u32[]{:S(2)}) %collective-permute-start) | collective-permute-done | bytes 917536 | tf_op jit(solution)/shard_map/ppermute | solution.py:312
  107.1 1.0 copy-done.4
  108.0 14.4 %shard_map.91 = (bf16[256,1792]{1,0:T(8,128)(2,1)}, bf16[256,1792]{1,0:T(8,128)(2,1)}) custom-call(s32[1]{0:T(128)} %bitcast.core, bf16[2,256,1792]{2,1,0:T(8,128)(2,1)} %bitcast.23, bf16[256,1792]{1,0:T(8,128)(2,1)} %copy-done.4, bf16[3584,512]{1,0:T(8,128)(2,1)} %bitcast.30, bf16[3584,512]{1,0:T(8,128)(2,1)} %bitcast.33, bf16[512,3584]{1,0:T(8,128)(2,1)} %bitcast.36, ...), custom_call_target="tpu_custom_call" | custom-call | flops 5637144576 | bytes 25690112 | tf_op jit(solution)/shard_map/pallas_call | solution.py:194
  122.4 0.1 collective-permute-start.4
  122.6 2.6 %collective-permute-done.4 = bf16[256,1792]{1,0:T(8,128)(2,1)S(1)} collective-permute-done((bf16[256,1792]{1,0:T(8,128)(2,1)}, bf16[256,1792]{1,0:T(8,128)(2,1)S(1)}, u32[]{:S(2)}, u32[]{:S(2)}) %collective-permute-start.4) | collective-permute-done | bytes 917536 | tf_op jit(solution)/shard_map/ppermute | solution.py:314
  125.1 3.1 %maximum_select_fusion = bf16[2,256,1792]{2,1,0:T(8,128)(2,1)} fusion(bf16[1,256,1792]{2,1,0:T(8,128)(2,1)S(1)} %bitcast.38, bf16[1,256,1792]{2,1,0:T(8,128)(2,1)} %bitcast.37, pred[]{:T(512)S(6)} %eq.3), kind=kLoop, calls=%fused_computation | loop fusion | flops 2752512 | bytes 3670017 | tf_op jit(solution)/shard_map/jit(_where)/select_n | solution.py:315
  128.3 21.9 %all-to-all-done.3 = bf16[64,8,3584]{2,1,0:T(8,128)(2,1)} async-done(((bf16[64,8,3584]{2,1,0:T(8,128)(2,1)}), bf16[64,8,3584]{2,1,0:T(8,128)(2,1)}, u32[]{:S(2)}, u32[]{:S(2)}) %all-to-all-start.3) | async-done | bytes 3670048 | tf_op jit(solution)/shard_map/all_to_all | solution.py:289
  150.1 5.0 %all-to-all-start.1 = ((bf16[64,8,1792]{2,1,0:T(8,128)(2,1)}), bf16[64,8,1792]{2,1,0:T(8,128)(2,1)S(1)}, u32[]{:S(2)}, u32[]{:S(2)}) async-start(bf16[64,8,1792]{2,1,0:T(8,128)(2,1)} %bitcast.25), calls=%async_computation.1 | async-start | bytes 3670016 | tf_op jit(solution)/shard_map/all_to_all | solution.py:289
  155.1 0.7 copy.11.gates
  155.8 2.7 %weight_tables.1 = (bf16[256,512]{1,0:T(8,128)(2,1)}, bf16[256,512]{1,0:T(8,128)(2,1)}) custom-call(s32[1]{0:T(128)} %bitcast.core, s32[128,8]{1,0:T(8,128)} %copy.10.ids, f32[128,8]{1,0:T(8,128)} %copy.11.gates), custom_call_target="tpu_custom_call" | custom-call | tf_op jit(solution)/shard_map/weight_tables/pallas_call | solution.py:107
  158.5 2.7 %fusion.9 = f32[128,512]{1,0:T(8,128)S(1)} fusion(bf16[128,3584]{1,0:T(8,128)(2,1)S(1)} %copy-done, bf16[3584,512]{1,0:T(8,128)(2,1)} %param.15), kind=kOutput, calls=%fused_computation.12 | convolution fusion | flops 469762048 | bytes 4849664 | tf_op jit(solution)/shard_map/dot_general | solution.py:282
  161.2 5.7 %fusion.1.shared = f32[128,3584]{1,0:T(8,128)} fusion(bf16[512,3584]{1,0:T(8,128)(2,1)} %param.17, bf16[128,3584]{1,0:T(8,128)(2,1)S(1)} %copy-done, bf16[3584,512]{1,0:T(8,128)(2,1)} %param.16, f32[128,512]{1,0:T(8,128)S(1)} %fusion.9), kind=kOutput, calls=%fused_computation.3 | convolution fusion | flops 939917312 | bytes 10354688 | tf_op jit(solution)/shard_map/dot_general | solution.py:285
  166.9 5.4 %combine_head.1 = (f32[128,1792]{1,0:T(8,128)}, f32[128,1792]{1,0:T(8,128)}) custom-call(s32[1]{0:T(128)} %bitcast.core, bf16[256,512]{1,0:T(8,128)(2,1)} %get-tuple-element.14.table, bf16[512,3584]{1,0:T(8,128)(2,1)} %bitcast.14.rows, f32[128,3584]{1,0:T(8,128)} %fusion.1.shared), custom_call_target="tpu_custom_call" | custom-call | tf_op jit(solution)/shard_map/combine_head/pallas_call | solution.py:237
  172.3 8.9 %all-to-all-done.1 = bf16[64,8,1792]{2,1,0:T(8,128)(2,1)S(1)} async-done(((bf16[64,8,1792]{2,1,0:T(8,128)(2,1)}), bf16[64,8,1792]{2,1,0:T(8,128)(2,1)S(1)}, u32[]{:S(2)}, u32[]{:S(2)}) %all-to-all-start.1) | async-done | bytes 1835040 | tf_op jit(solution)/shard_map/all_to_all | solution.py:289
  181.2 1.3 copy-done.2
  182.4 0.3 copy-done.3
  182.7 3.3 %combine_tail.1 = bf16[128,1792]{1,0:T(8,128)(2,1)} custom-call(bf16[256,512]{1,0:T(8,128)(2,1)} %get-tuple-element.11.table, bf16[512,1792]{1,0:T(8,128)(2,1)} %bitcast.24, f32[128,1792]{1,0:T(8,128)} %get-tuple-element.15.keep, f32[128,1792]{1,0:T(8,128)} %copy-done.3), custom_call_target="tpu_custom_call" | custom-call | tf_op jit(solution)/shard_map/combine_tail/pallas_call | solution.py:266
  (13 shorter events, 0.0 us)
Async XLA Ops:
  6.6 60.1 %all-to-all-start.2 = ((bf16[64,8,3584]{2,1,0:T(8,128)(2,1)}), bf16[64,8,3584]{2,1,0:T(8,128)(2,1)}, u32[]{:S(2)}, u32[]{:S(2)}) async-start(bf16[64,8,3584]{2,1,0:T(8,128)(2,1)} %bitcast.21), calls=%async_computation.2 | async-start | bytes 7340032 | tf_op jit(solution)/shard_map/all_to_all | solution.py:289
  18.4 53.5 %collective-permute-start.1 = (bf16[3584,512]{1,0:T(8,128)(2,1)}, bf16[3584,512]{1,0:T(8,128)(2,1)}, u32[]{:S(2)}, u32[]{:S(2)}) collective-permute-start(bf16[3584,512]{1,0:T(8,128)(2,1)} %bitcast.28), channel_id=1, source_target_pairs={{0,1},{1,0},{2,3},{3,2},{4,5},{5,4},{6,7},{7,6},{8,9},{9,8},{10,11... | collective-permute-start | bytes 11010056 | tf_op jit(solution)/shard_map/ppermute | solution.py:301
  18.5 53.4 %collective-permute-start.2 = (bf16[3584,512]{1,0:T(8,128)(2,1)}, bf16[3584,512]{1,0:T(8,128)(2,1)}, u32[]{:S(2)}, u32[]{:S(2)}) collective-permute-start(bf16[3584,512]{1,0:T(8,128)(2,1)} %bitcast.31), channel_id=1, source_target_pairs={{0,1},{1,0},{2,3},{3,2},{4,5},{5,4},{6,7},{7,6},{8,9},{9,8},{10,11... | collective-permute-start | bytes 11010056 | tf_op jit(solution)/shard_map/ppermute | solution.py:301
  19.0 52.9 %collective-permute-start.3 = (bf16[512,3584]{1,0:T(8,128)(2,1)}, bf16[512,3584]{1,0:T(8,128)(2,1)}, u32[]{:S(2)}, u32[]{:S(2)}) collective-permute-start(bf16[512,3584]{1,0:T(8,128)(2,1)} %bitcast.34), channel_id=1, source_target_pairs={{0,1},{1,0},{2,3},{3,2},{4,5},{5,4},{6,7},{7,6},{8,9},{9,8},{10,11... | collective-permute-start | bytes 11010056 | tf_op jit(solution)/shard_map/ppermute | solution.py:301
  66.7 31.9 %all-to-all-start = ((bf16[64,8,1792]{2,1,0:T(8,128)(2,1)}), bf16[64,8,1792]{2,1,0:T(8,128)(2,1)S(1)}, u32[]{:S(2)}, u32[]{:S(2)}) async-start(bf16[64,8,1792]{2,1,0:T(8,128)(2,1)} %bitcast.26), calls=%async_computation | async-start | bytes 3670016 | tf_op jit(solution)/shard_map/all_to_all | solution.py:289
  98.6 5.8 %copy-start.1 = (bf16[64,8,1792]{2,1,0:T(8,128)(2,1)}, bf16[64,8,1792]{2,1,0:T(8,128)(2,1)S(1)}, u32[]{:S(2)}) copy-start(bf16[64,8,1792]{2,1,0:T(8,128)(2,1)S(1)} %all-to-all-done) | copy-start | bytes 5505028
  98.6 51.5 %all-to-all-start.3 = ((bf16[64,8,3584]{2,1,0:T(8,128)(2,1)}), bf16[64,8,3584]{2,1,0:T(8,128)(2,1)}, u32[]{:S(2)}, u32[]{:S(2)}) async-start(bf16[64,8,3584]{2,1,0:T(8,128)(2,1)} %bitcast.27), calls=%async_computation.3 | async-start | bytes 7340032 | tf_op jit(solution)/shard_map/all_to_all | solution.py:289
  104.5 2.6 %collective-permute-start = (bf16[256,1792]{1,0:T(8,128)(2,1)S(1)}, bf16[256,1792]{1,0:T(8,128)(2,1)S(1)}, u32[]{:S(2)}, u32[]{:S(2)}) collective-permute-start(bf16[256,1792]{1,0:T(8,128)(2,1)S(1)} %dynamic-slice_bitcast_fusion), channel_id=1, source_target_pairs={{0,1},{1,0},{2,3},{3,2},{4,5},{5,4},{6,7},{7,6},{8,9},{9,8},{10,11... | collective-permute-start | bytes 2752520 | tf_op jit(solution)/shard_map/ppermute | solution.py:312
  107.1 1.0 copy-start.4
  122.4 2.7 %collective-permute-start.4 = (bf16[256,1792]{1,0:T(8,128)(2,1)}, bf16[256,1792]{1,0:T(8,128)(2,1)S(1)}, u32[]{:S(2)}, u32[]{:S(2)}) collective-permute-start(bf16[256,1792]{1,0:T(8,128)(2,1)} %get-tuple-element.13), channel_id=1, source_target_pairs={{0,1},{1,0},{2,3},{3,2},{4,5},{5,4},{6,7},{7,6},{8,9},{9,8},{10,11... | collective-permute-start | bytes 2752520 | tf_op jit(solution)/shard_map/ppermute | solution.py:314
  125.1 30.0 %copy-start.5 = (f32[128,8]{0,1:T(8,128)S(1)}, f32[128,8]{0,1:T(8,128)}, u32[]{:S(2)}) copy-start(f32[128,8]{0,1:T(8,128)} %param.11) | copy-start | bytes 12292
  125.1 33.4 %copy-start = (bf16[128,3584]{1,0:T(8,128)(2,1)S(1)}, bf16[128,3584]{1,0:T(8,128)(2,1)}, u32[]{:S(2)}) copy-start(bf16[128,3584]{1,0:T(8,128)(2,1)} %tokens.3) | copy-start | bytes 2752516
  150.1 31.1 %all-to-all-start.1 = ((bf16[64,8,1792]{2,1,0:T(8,128)(2,1)}), bf16[64,8,1792]{2,1,0:T(8,128)(2,1)S(1)}, u32[]{:S(2)}, u32[]{:S(2)}) async-start(bf16[64,8,1792]{2,1,0:T(8,128)(2,1)} %bitcast.25), calls=%async_computation.1 | async-start | bytes 3670016 | tf_op jit(solution)/shard_map/all_to_all | solution.py:289
  172.3 8.9 %collective-permute-start.5 = (f32[128,1792]{1,0:T(8,128)}, f32[128,1792]{1,0:T(8,128)S(1)}, u32[]{:S(2)}, u32[]{:S(2)}) collective-permute-start(f32[128,1792]{1,0:T(8,128)} %get-tuple-element.16), channel_id=1, source_target_pairs={{0,1},{1,0},{2,3},{3,2},{4,5},{5,4},{6,7},{7,6},{8,9},{9,8},{10,11... | collective-permute-start | bytes 2752520 | tf_op jit(solution)/shard_map/ppermute | solution.py:318
  181.2 1.3 copy-start.2
  181.2 1.5 copy-start.3

commit v2 on v1

--- a/solution.py
+++ b/solution.py
@@ -12,7 +12,6 @@
 TILE = 8
 F32 = jnp.float32
 BF16 = jnp.bfloat16
-NT = (((1,), (1,)), ((), ()))
 
 
 def named(ids, experts):
@@ -33,12 +32,20 @@
 
 
 def pick_rows(ids, experts, first):
-    rank, _ = ranks(ids, experts)
+    top, rows = ids.shape
+    row = lax.broadcasted_iota(jnp.int32, (experts, rows), 0)
+    hits = [(ids[k : k + 1, :] == row).astype(F32) for k in range(top)]
+    chosen = functools.reduce(jnp.add, hits)
+    earlier = lax.broadcasted_iota(jnp.int32, (rows, rows), 0)
+    later = lax.broadcasted_iota(jnp.int32, (rows, rows), 1)
+    before = (earlier < later).astype(F32).astype(BF16)
+    rank = jnp.dot(chosen.astype(BF16), before, preferred_element_type=F32)
+    rank = jnp.where(chosen > 0, rank, -1.0)
     count = experts * TILE
     slot = lax.broadcasted_iota(jnp.int32, (count, experts), 0)
     expert = lax.broadcasted_iota(jnp.int32, (count, experts), 1)
     spread = (lax.shift_right_logical(slot, 3) == expert).astype(F32).astype(BF16)
-    wide = lax.dot_general(spread, rank.astype(BF16), NT, preferred_element_type=F32)
+    wide = jnp.dot(spread, rank.astype(BF16), preferred_element_type=F32)
     place = lax.broadcasted_iota(jnp.int32, wide.shape, 0) & (TILE - 1)
     return (wide == (place + first).astype(F32)).astype(F32).astype(BF16)
 
@@ -65,34 +72,78 @@
     return jnp.concatenate(parts, axis=0)
 
 
-def dispatch_body(experts, tail, core, ids, tokens, out, picks):
+VMEM = pl.BlockSpec(memory_space=pltpu.VMEM)
+SMEM = pl.BlockSpec(memory_space=pltpu.SMEM)
+
+
+HBM = pl.BlockSpec(memory_space=pl.ANY)
+CHUNKS = 4
+
+
+def dispatch_head_body(experts, core, ids, tokens, out, source, rows, loads, stores):
+    block = source.shape[2]
+    span = lambda j: pl.ds(j * block, block)
+    fetch = [
+        pltpu.make_async_copy(tokens.at[:, span(j)], source.at[j], loads.at[j])
+        for j in range(CHUNKS)
+    ]
+    write = [
+        pltpu.make_async_copy(rows.at[j], out.at[:, span(j)], stores.at[j]) for j in range(CHUNKS)
+    ]
+    for copy in fetch:
+        copy.start()
+    picks = pick_rows(ids[...], experts, core[0] * TILE)
+    for j in range(CHUNKS):
+        fetch[j].wait()
+        rows[j] = jnp.dot(picks, source[j], preferred_element_type=F32).astype(BF16)
+        write[j].start()
+    for copy in write:
+        copy.wait()
+
+
+def dispatch_head(core, ids, tokens, experts):
+    count, width = tokens.shape
+    block = width // CHUNKS
+    return pl.pallas_call(
+        functools.partial(dispatch_head_body, experts),
+        out_shape=jax.ShapeDtypeStruct((experts * TILE, width), BF16),
+        in_specs=[SMEM, VMEM, HBM],
+        out_specs=HBM,
+        scratch_shapes=[
+            pltpu.VMEM((CHUNKS, count, block), BF16),
+            pltpu.VMEM((CHUNKS, experts * TILE, block), BF16),
+            pltpu.SemaphoreType.DMA((CHUNKS,)),
+            pltpu.SemaphoreType.DMA((CHUNKS,)),
+        ],
+        name="dispatch_head",
+    )(core, ids, tokens)
+
+
+def dispatch_tail_body(experts, core, ids, tokens, out, picks):
     @pl.when(pl.program_id(0) == 0)
     def _():
-        first = 2 * TILE if tail else core[0] * TILE
-        picks[...] = pick_rows(ids[...], experts, first)
+        picks[...] = pick_rows(ids[...], experts, 2 * TILE)
 
     out[...] = jnp.dot(picks[...], tokens[...], preferred_element_type=F32).astype(BF16)
 
 
-def dispatch(core, ids, tokens, experts, tail):
+def dispatch_tail(core, ids, tokens, experts):
     rows, width = tokens.shape
     block = width // 4
-    steps = 2 if tail else 4
-    column = (lambda i, c: (0, 2 * c[0] + i)) if tail else (lambda i, c: (0, i))
-    return pl.pallas_call(
-        functools.partial(dispatch_body, experts, tail),
-        out_shape=jax.ShapeDtypeStruct((experts * TILE, steps * block), BF16),
+    return pl.pallas_call(
+        functools.partial(dispatch_tail_body, experts),
+        out_shape=jax.ShapeDtypeStruct((experts * TILE, 2 * block), BF16),
         grid_spec=pltpu.PrefetchScalarGridSpec(
             num_scalar_prefetch=1,
-            grid=(steps,),
+            grid=(2,),
             in_specs=[
                 pl.BlockSpec(ids.shape, lambda i, c: (0, 0)),
-                pl.BlockSpec((rows, block), column),
+                pl.BlockSpec((rows, block), lambda i, c: (0, 2 * c[0] + i)),
             ],
             out_specs=pl.BlockSpec((experts * TILE, block), lambda i, c: (0, i)),
             scratch_shapes=[pltpu.VMEM((experts * TILE, rows), BF16)],
         ),
-        name="dispatch_tail" if tail else "dispatch_head",
+        name="dispatch_tail",
     )(core, ids, tokens)
 
 
@@ -250,6 +301,7 @@
                 pl.BlockSpec((tokens, block), lambda i, c: (0, jnp.maximum(i - 2, 0))),
             ),
         ),
+        compiler_params=pltpu.CompilerParams(vmem_limit_bytes=24 << 20),
         name="combine_head",
     )(core, table, rows, shared)
 
@@ -260,22 +312,14 @@
 
 
 def combine_tail(table, rows, keep, received):
-    count, width = rows.shape
-    tokens = keep.shape[0]
-    block = width // 2
     return pl.pallas_call(
         combine_tail_body,
-        out_shape=jax.ShapeDtypeStruct((tokens, width), BF16),
-        grid=(2,),
-        in_specs=[
-            pl.BlockSpec(table.shape, lambda i: (0, 0)),
-            pl.BlockSpec((count, block), lambda i: (0, i)),
-            pl.BlockSpec((tokens, block), lambda i: (0, i)),
-            pl.BlockSpec((tokens, block), lambda i: (0, i)),
-        ],
-        out_specs=pl.BlockSpec((tokens, block), lambda i: (0, i)),
+        out_shape=jax.ShapeDtypeStruct(keep.shape, BF16),
+        in_specs=[VMEM] * 4,
+        out_specs=VMEM,
+        compiler_params=pltpu.CompilerParams(vmem_limit_bytes=24 << 20),
         name="combine_tail",
-    )(table, rows, keep, received)
+    )(*[pltpu.with_memory_space_constraint(v, pltpu.VMEM) for v in (table, rows, keep, received)])
 
 
 def shared_apply(inputs, gate_matrix, up_matrix, down_matrix):
@@ -299,9 +343,10 @@
     swap = [(0, 1), (1, 0)]
     own = (w_gate[0], w_up[0], w_down[0])
     other = tuple(lax.ppermute(w, "tp", swap) for w in own)
-    head = dispatch(core, expert_ids, tokens, experts, False)
+    ids = expert_ids.T
+    head = dispatch_head(core, ids, tokens, experts)
     head_in = exchange(head.reshape(experts, TILE, width), "ep")
-    tail = dispatch(core, expert_ids, tokens, experts, True)
+    tail = dispatch_tail(core, ids, tokens, experts)
     tail_in = exchange(tail.reshape(experts, TILE, half), "ep")
     table_head, table_tail = tables(core, expert_ids, gate_values, experts)
     shared = shared_apply(tokens, shared_gate, shared_up, shared_down)

time: 187 us -> 183 us (0.979)
  local copies, waits for them, and re-layouts: 4.73 us -> 2.47 us
  Pallas kernels: 54.7 us -> 52.8 us
    unnamed x14 -> x16, local copies, waits for them, and re-layouts: 4.66 us -> 2.4 us
  transfers between devices with their start and end apart: 10 -> 10, of which waited for: 6 -> 6; matrix products, arithmetic and copies ran while one was open for 7% -> 6% of each run, Pallas kernels for 25% -> 25%
where the time goes in v2:
time: 183 us; the launch traced here: 182 us
  waiting for transfers between devices  87.3 us (48%)
  Pallas kernels  52.8 us (29%)
  starting transfers between devices  29.1 us (16%)
  matrix products  7.1 us (4%)
  other arithmetic  3.12 us (2%)
  local copies, waits for them, and re-layouts  2.47 us (1%)
    all_to_all x4, waiting for transfers between devices, exchange(): return lax.all_to_all(x, axis, split_axis=0, concat_axis=0, tiled=True)  82.2 us
    pallas_call x2, Pallas kernels, expert_apply(): pl.pallas_call(functools.partial(body, steps), out_shape=out, grid_spec=p...  34.8 us
    all_to_all x4, starting transfers between devices, exchange(): return lax.all_to_all(x, axis, split_axis=0, concat_axis=0, tiled=True)  28.2 us
    pallas_call x1, Pallas kernels, combine_head(): pl.pallas_call(combine_head_body, out_shape=(out, out), grid_spec=pltpu.P...  5.04 us
    dot_general x1, matrix products, shared_apply(): return jnp.dot(hidden, down_matrix, preferred_element_type=F32)  4.43 us
    pallas_call x1, Pallas kernels, dispatch_head(): pl.pallas_call(functools.partial(dispatch_head_body, experts), out_shape=...  4.35 us
  transfers between devices with their start and end apart: 10, of which 6 were waited for; matrix products, arithmetic and copies ran while one was open for 6% of the time, Pallas kernels for 25%

profile of v2, /device:TPU:0, one launch (start us, length us, event | category | flops | bytes accessed | tf_op | source)
XLA Modules:
  0.0 182.1 jit_solution(1262090237035179762)
XLA Ops:
  0.0 4.3 %dispatch_head.1 = bf16[512,3584]{1,0:T(8,128)(2,1)} custom-call(s32[1]{0:T(128)} %bitcast.core, s32[8,128]{1,0:T(8,128)} %bitcast.38, bf16[128,3584]{1,0:T(8,128)(2,1)} %tokens.3), custom_call_target="tpu_custom_call" | custom-call | tf_op jit(solution)/shard_map/dispatch_head/pallas_call | solution.py:107
  4.4 11.8 %all-to-all-start.2 = ((bf16[64,8,3584]{2,1,0:T(8,128)(2,1)}), bf16[64,8,3584]{2,1,0:T(8,128)(2,1)}, u32[]{:S(2)}, u32[]{:S(2)}) async-start(bf16[64,8,3584]{2,1,0:T(8,128)(2,1)} %bitcast.22), calls=%async_computation.2 | async-start | bytes 7340032 | tf_op jit(solution)/shard_map/all_to_all | solution.py:333
  16.1 0.1 collective-permute-start.1
  16.2 0.5 collective-permute-start.2
  16.7 0.1 collective-permute-start.3
  16.8 3.1 %dispatch_tail.1 = bf16[512,1792]{1,0:T(8,128)(2,1)} custom-call(s32[1]{0:T(128)} %bitcast.core, s32[8,128]{1,0:T(8,128)} %bitcast.39, bf16[128,3584]{1,0:T(8,128)(2,1)} %tokens.3), custom_call_target="tpu_custom_call" | custom-call | tf_op jit(solution)/shard_map/dispatch_tail/pallas_call | solution.py:133
  19.9 44.6 %all-to-all-done.2 = bf16[64,8,3584]{2,1,0:T(8,128)(2,1)} async-done(((bf16[64,8,3584]{2,1,0:T(8,128)(2,1)}), bf16[64,8,3584]{2,1,0:T(8,128)(2,1)}, u32[]{:S(2)}, u32[]{:S(2)}) %all-to-all-start.2) | async-done | bytes 3670048 | tf_op jit(solution)/shard_map/all_to_all | solution.py:333
  64.5 5.2 %all-to-all-start = ((bf16[64,8,1792]{2,1,0:T(8,128)(2,1)}), bf16[64,8,1792]{2,1,0:T(8,128)(2,1)S(1)}, u32[]{:S(2)}, u32[]{:S(2)}) async-start(bf16[64,8,1792]{2,1,0:T(8,128)(2,1)} %bitcast.25), calls=%async_computation | async-start | bytes 3670016 | tf_op jit(solution)/shard_map/all_to_all | solution.py:333
  69.6 0.0 collective-permute-done.1.g1
  69.7 0.0 collective-permute-done.2.u1
  69.7 20.3 %shard_map.92 = bf16[512,3584]{1,0:T(8,128)(2,1)} custom-call(s32[1]{0:T(128)} %bitcast.core, bf16[512,3584]{1,0:T(8,128)(2,1)} %bitcast.13.x, bf16[3584,512]{1,0:T(8,128)(2,1)} %bitcast.28, bf16[3584,512]{1,0:T(8,128)(2,1)} %bitcast.31, bf16[512,3584]{1,0:T(8,128)(2,1)} %bitcast.34, bf16[3584,512]{1,0:T(8,128)(2,1)} %collective-permute-done.1.g1, ...), custom_call_target="tpu_custom_call" | custom-call | flops 11274289152 | bytes 29360128 | tf_op jit(solution)/shard_map/pallas_call | solution.py:245
  90.0 6.3 %all-to-all-done = bf16[64,8,1792]{2,1,0:T(8,128)(2,1)S(1)} async-done(((bf16[64,8,1792]{2,1,0:T(8,128)(2,1)}), bf16[64,8,1792]{2,1,0:T(8,128)(2,1)S(1)}, u32[]{:S(2)}, u32[]{:S(2)}) %all-to-all-start) | async-done | bytes 1835040 | tf_op jit(solution)/shard_map/all_to_all | solution.py:333
  96.3 5.8 %all-to-all-start.3 = ((bf16[64,8,3584]{2,1,0:T(8,128)(2,1)}), bf16[64,8,3584]{2,1,0:T(8,128)(2,1)}, u32[]{:S(2)}, u32[]{:S(2)}) async-start(bf16[64,8,3584]{2,1,0:T(8,128)(2,1)} %bitcast.26), calls=%async_computation.3 | async-start | bytes 7340032 | tf_op jit(solution)/shard_map/all_to_all | solution.py:333
  102.2 0.1 dynamic-slice_bitcast_fusion
  102.2 0.1 collective-permute-start
  102.3 2.5 %collective-permute-done.x1 = bf16[256,1792]{1,0:T(8,128)(2,1)S(1)} collective-permute-done((bf16[256,1792]{1,0:T(8,128)(2,1)S(1)}, bf16[256,1792]{1,0:T(8,128)(2,1)S(1)}, u32[]{:S(2)}, u32[]{:S(2)}) %collective-permute-start) | collective-permute-done | bytes 917536 | tf_op jit(solution)/shard_map/ppermute | solution.py:357
  104.8 0.9 copy-done.4
  105.7 14.4 %shard_map.91 = (bf16[256,1792]{1,0:T(8,128)(2,1)}, bf16[256,1792]{1,0:T(8,128)(2,1)}) custom-call(s32[1]{0:T(128)} %bitcast.core, bf16[2,256,1792]{2,1,0:T(8,128)(2,1)} %bitcast.24, bf16[256,1792]{1,0:T(8,128)(2,1)} %copy-done.4, bf16[3584,512]{1,0:T(8,128)(2,1)} %bitcast.29, bf16[3584,512]{1,0:T(8,128)(2,1)} %bitcast.32, bf16[512,3584]{1,0:T(8,128)(2,1)} %bitcast.35, ...), custom_call_target="tpu_custom_call" | custom-call | flops 5637144576 | bytes 25690112 | tf_op jit(solution)/shard_map/pallas_call | solution.py:245
  120.2 0.1 collective-permute-start.4
  120.3 2.6 %collective-permute-done.4 = bf16[256,1792]{1,0:T(8,128)(2,1)S(1)} collective-permute-done((bf16[256,1792]{1,0:T(8,128)(2,1)}, bf16[256,1792]{1,0:T(8,128)(2,1)S(1)}, u32[]{:S(2)}, u32[]{:S(2)}) %collective-permute-start.4) | collective-permute-done | bytes 917536 | tf_op jit(solution)/shard_map/ppermute | solution.py:359
  122.8 3.1 %maximum_select_fusion = bf16[2,256,1792]{2,1,0:T(8,128)(2,1)} fusion(bf16[1,256,1792]{2,1,0:T(8,128)(2,1)S(1)} %bitcast.37, bf16[1,256,1792]{2,1,0:T(8,128)(2,1)} %bitcast.36, pred[]{:T(512)S(6)} %eq.3), kind=kLoop, calls=%fused_computation | loop fusion | flops 2752512 | bytes 3670017 | tf_op jit(solution)/shard_map/jit(_where)/select_n | solution.py:360
  126.0 21.9 %all-to-all-done.3 = bf16[64,8,3584]{2,1,0:T(8,128)(2,1)} async-done(((bf16[64,8,3584]{2,1,0:T(8,128)(2,1)}), bf16[64,8,3584]{2,1,0:T(8,128)(2,1)}, u32[]{:S(2)}, u32[]{:S(2)}) %all-to-all-start.3) | async-done | bytes 3670048 | tf_op jit(solution)/shard_map/all_to_all | solution.py:333
  147.9 5.5 %all-to-all-start.1 = ((bf16[64,8,1792]{2,1,0:T(8,128)(2,1)}), bf16[64,8,1792]{2,1,0:T(8,128)(2,1)}, u32[]{:S(2)}, u32[]{:S(2)}) async-start(bf16[64,8,1792]{2,1,0:T(8,128)(2,1)} %bitcast.10), calls=%async_computation.1 | async-start | bytes 3670016 | tf_op jit(solution)/shard_map/all_to_all | solution.py:333
  153.4 0.7 copy.10.ids
  154.2 0.7 copy.11.gates
  154.9 2.7 %weight_tables.1 = (bf16[256,512]{1,0:T(8,128)(2,1)}, bf16[256,512]{1,0:T(8,128)(2,1)}) custom-call(s32[1]{0:T(128)} %bitcast.core, s32[128,8]{1,0:T(8,128)} %copy.10.ids, f32[128,8]{1,0:T(8,128)} %copy.11.gates), custom_call_target="tpu_custom_call" | custom-call | tf_op jit(solution)/shard_map/weight_tables/pallas_call | solution.py:158
  157.6 2.7 %fusion.9 = f32[128,512]{1,0:T(8,128)S(1)} fusion(bf16[128,3584]{1,0:T(8,128)(2,1)S(1)} %copy-done.2, bf16[3584,512]{1,0:T(8,128)(2,1)} %param.15), kind=kOutput, calls=%fused_computation.12 | convolution fusion | flops 469762048 | bytes 4849664 | tf_op jit(solution)/shard_map/dot_general | solution.py:326
  160.3 0.0 copy-start.1
  160.3 4.4 %fusion.1.shared = f32[128,3584]{1,0:T(8,128)S(1)} fusion(bf16[512,3584]{1,0:T(8,128)(2,1)} %param.17, bf16[128,3584]{1,0:T(8,128)(2,1)S(1)} %copy-done.2, bf16[3584,512]{1,0:T(8,128)(2,1)} %param.16, f32[128,512]{1,0:T(8,128)S(1)} %fusion.9), kind=kOutput, calls=%fused_computation.3 | convolution fusion | flops 939917312 | bytes 10354688 | tf_op jit(solution)/shard_map/dot_general | solution.py:329
  164.8 5.0 %combine_head.1 = (f32[128,1792]{1,0:T(8,128)}, f32[128,1792]{1,0:T(8,128)S(1)}) custom-call(s32[1]{0:T(128)} %bitcast.core, bf16[256,512]{1,0:T(8,128)(2,1)S(1)} %copy-done.1, bf16[512,3584]{1,0:T(8,128)(2,1)} %bitcast.15.rows, f32[128,3584]{1,0:T(8,128)S(1)} %fusion.1.shared), custom_call_target="tpu_custom_call" | custom-call | tf_op jit(solution)/shard_map/combine_head/pallas_call | solution.py:288
  169.8 9.4 %all-to-all-done.1 = bf16[64,8,1792]{2,1,0:T(8,128)(2,1)} async-done(((bf16[64,8,1792]{2,1,0:T(8,128)(2,1)}), bf16[64,8,1792]{2,1,0:T(8,128)(2,1)}, u32[]{:S(2)}, u32[]{:S(2)}) %all-to-all-start.1) | async-done | bytes 1835040 | tf_op jit(solution)/shard_map/all_to_all | solution.py:333
  179.2 2.9 %combine_tail.1 = bf16[128,1792]{1,0:T(8,128)(2,1)} custom-call(bf16[256,512]{1,0:T(8,128)(2,1)S(1)} %copy-done, bf16[512,1792]{1,0:T(8,128)(2,1)} %bitcast.11.rows, f32[128,1792]{1,0:T(8,128)S(1)} %get-tuple-element.15.keep, f32[128,1792]{1,0:T(8,128)S(1)} %collective-permute-done.5.received), custom_call_target="tpu_custom_call" | custom-call | tf_op jit(solution)/shard_map/combine_tail/pallas_call | solution.py:315
  (15 shorter events, 0.0 us)
Async XLA Ops:
  4.4 60.1 %all-to-all-start.2 = ((bf16[64,8,3584]{2,1,0:T(8,128)(2,1)}), bf16[64,8,3584]{2,1,0:T(8,128)(2,1)}, u32[]{:S(2)}, u32[]{:S(2)}) async-start(bf16[64,8,3584]{2,1,0:T(8,128)(2,1)} %bitcast.22), calls=%async_computation.2 | async-start | bytes 7340032 | tf_op jit(solution)/shard_map/all_to_all | solution.py:333
  16.1 53.5 %collective-permute-start.1 = (bf16[3584,512]{1,0:T(8,128)(2,1)}, bf16[3584,512]{1,0:T(8,128)(2,1)}, u32[]{:S(2)}, u32[]{:S(2)}) collective-permute-start(bf16[3584,512]{1,0:T(8,128)(2,1)} %bitcast.27), channel_id=1, source_target_pairs={{0,1},{1,0},{2,3},{3,2},{4,5},{5,4},{6,7},{7,6},{8,9},{9,8},{10,11... | collective-permute-start | bytes 11010056 | tf_op jit(solution)/shard_map/ppermute | solution.py:345
  16.2 53.4 %collective-permute-start.2 = (bf16[3584,512]{1,0:T(8,128)(2,1)}, bf16[3584,512]{1,0:T(8,128)(2,1)}, u32[]{:S(2)}, u32[]{:S(2)}) collective-permute-start(bf16[3584,512]{1,0:T(8,128)(2,1)} %bitcast.30), channel_id=1, source_target_pairs={{0,1},{1,0},{2,3},{3,2},{4,5},{5,4},{6,7},{7,6},{8,9},{9,8},{10,11... | collective-permute-start | bytes 11010056 | tf_op jit(solution)/shard_map/ppermute | solution.py:345
  16.7 52.9 %collective-permute-start.3 = (bf16[512,3584]{1,0:T(8,128)(2,1)}, bf16[512,3584]{1,0:T(8,128)(2,1)}, u32[]{:S(2)}, u32[]{:S(2)}) collective-permute-start(bf16[512,3584]{1,0:T(8,128)(2,1)} %bitcast.33), channel_id=1, source_target_pairs={{0,1},{1,0},{2,3},{3,2},{4,5},{5,4},{6,7},{7,6},{8,9},{9,8},{10,11... | collective-permute-start | bytes 11010056 | tf_op jit(solution)/shard_map/ppermute | solution.py:345
  64.5 31.9 %all-to-all-start = ((bf16[64,8,1792]{2,1,0:T(8,128)(2,1)}), bf16[64,8,1792]{2,1,0:T(8,128)(2,1)S(1)}, u32[]{:S(2)}, u32[]{:S(2)}) async-start(bf16[64,8,1792]{2,1,0:T(8,128)(2,1)} %bitcast.25), calls=%async_computation | async-start | bytes 3670016 | tf_op jit(solution)/shard_map/all_to_all | solution.py:333
  96.3 5.8 %copy-start.3 = (bf16[64,8,1792]{2,1,0:T(8,128)(2,1)}, bf16[64,8,1792]{2,1,0:T(8,128)(2,1)S(1)}, u32[]{:S(2)}) copy-start(bf16[64,8,1792]{2,1,0:T(8,128)(2,1)S(1)} %all-to-all-done) | copy-start | bytes 5505028
  96.3 51.6 %all-to-all-start.3 = ((bf16[64,8,3584]{2,1,0:T(8,128)(2,1)}), bf16[64,8,3584]{2,1,0:T(8,128)(2,1)}, u32[]{:S(2)}, u32[]{:S(2)}) async-start(bf16[64,8,3584]{2,1,0:T(8,128)(2,1)} %bitcast.26), calls=%async_computation.3 | async-start | bytes 7340032 | tf_op jit(solution)/shard_map/all_to_all | solution.py:333
  102.2 2.6 %collective-permute-start = (bf16[256,1792]{1,0:T(8,128)(2,1)S(1)}, bf16[256,1792]{1,0:T(8,128)(2,1)S(1)}, u32[]{:S(2)}, u32[]{:S(2)}) collective-permute-start(bf16[256,1792]{1,0:T(8,128)(2,1)S(1)} %dynamic-slice_bitcast_fusion), channel_id=1, source_target_pairs={{0,1},{1,0},{2,3},{3,2},{4,5},{5,4},{6,7},{7,6},{8,9},{9,8},{10,11... | collective-permute-start | bytes 2752520 | tf_op jit(solution)/shard_map/ppermute | solution.py:357
  104.8 0.9 copy-start.4
  120.2 2.7 %collective-permute-start.4 = (bf16[256,1792]{1,0:T(8,128)(2,1)}, bf16[256,1792]{1,0:T(8,128)(2,1)S(1)}, u32[]{:S(2)}, u32[]{:S(2)}) collective-permute-start(bf16[256,1792]{1,0:T(8,128)(2,1)} %get-tuple-element.13), channel_id=1, source_target_pairs={{0,1},{1,0},{2,3},{3,2},{4,5},{5,4},{6,7},{7,6},{8,9},{9,8},{10,11... | collective-permute-start | bytes 2752520 | tf_op jit(solution)/shard_map/ppermute | solution.py:359
  122.8 30.6 %copy-start.5 = (s32[128,8]{0,1:T(8,128)S(1)}, s32[128,8]{0,1:T(8,128)}, u32[]{:S(2)}) copy-start(s32[128,8]{0,1:T(8,128)} %param.10) | copy-start | bytes 12292
  122.8 31.3 %copy-start.6 = (f32[128,8]{0,1:T(8,128)S(1)}, f32[128,8]{0,1:T(8,128)}, u32[]{:S(2)}) copy-start(f32[128,8]{0,1:T(8,128)} %param.11) | copy-start | bytes 12292
  122.8 34.8 %copy-start.2 = (bf16[128,3584]{1,0:T(8,128)(2,1)S(1)}, bf16[128,3584]{1,0:T(8,128)(2,1)}, u32[]{:S(2)}) copy-start(bf16[128,3584]{1,0:T(8,128)(2,1)} %tokens.3) | copy-start | bytes 2752516
  147.9 31.3 %all-to-all-start.1 = ((bf16[64,8,1792]{2,1,0:T(8,128)(2,1)}), bf16[64,8,1792]{2,1,0:T(8,128)(2,1)}, u32[]{:S(2)}, u32[]{:S(2)}) async-start(bf16[64,8,1792]{2,1,0:T(8,128)(2,1)} %bitcast.10), calls=%async_computation.1 | async-start | bytes 3670016 | tf_op jit(solution)/shard_map/all_to_all | solution.py:333
  160.3 4.5 %copy-start.1 = (bf16[256,512]{1,0:T(8,128)(2,1)S(1)}, bf16[256,512]{1,0:T(8,128)(2,1)}, u32[]{:S(2)}) copy-start(bf16[256,512]{1,0:T(8,128)(2,1)} %get-tuple-element.14.table) | copy-start | bytes 786436
  164.7 14.5 %copy-start = (bf16[256,512]{1,0:T(8,128)(2,1)S(1)}, bf16[256,512]{1,0:T(8,128)(2,1)}, u32[]{:S(2)}) copy-start(bf16[256,512]{1,0:T(8,128)(2,1)} %get-tuple-element.11.table) | copy-start | bytes 786436
  169.8 9.4 %collective-permute-start.5 = (f32[128,1792]{1,0:T(8,128)}, f32[128,1792]{1,0:T(8,128)S(1)}, u32[]{:S(2)}, u32[]{:S(2)}) collective-permute-start(f32[128,1792]{1,0:T(8,128)} %get-tuple-element.16), channel_id=1, source_target_pairs={{0,1},{1,0},{2,3},{3,2},{4,5},{5,4},{6,7},{7,6},{8,9},{9,8},{10,11... | collective-permute-start | bytes 2752520 | tf_op jit(solution)/shard_map/ppermute | solution.py:363

commit v3 on v2

--- a/solution.py
+++ b/solution.py
@@ -77,7 +77,7 @@
 
 
 HBM = pl.BlockSpec(memory_space=pl.ANY)
-CHUNKS = 4
+CHUNKS = 7
 
 
 def dispatch_head_body(experts, core, ids, tokens, out, source, rows, loads, stores):
@@ -306,20 +306,45 @@
     )(core, table, rows, shared)
 
 
-def combine_tail_body(table, rows, keep, received, out):
-    value = weighted(table[...], rows[...]) + (keep[...] + received[...])
-    out[...] = value.astype(BF16)
+def combine_tail_body(table, rows, keep, received, out, source, value, loads, stores):
+    block = source.shape[2]
+    span = lambda j: pl.ds(j * block, block)
+    fetch = [
+        pltpu.make_async_copy(rows.at[:, span(j)], source.at[j], loads.at[j]) for j in range(CHUNKS)
+    ]
+    write = [
+        pltpu.make_async_copy(value.at[j], out.at[:, span(j)], stores.at[j]) for j in range(CHUNKS)
+    ]
+    for copy in fetch:
+        copy.start()
+    for j in range(CHUNKS):
+        fetch[j].wait()
+        total = weighted(table[...], source[j]) + (keep[:, span(j)] + received[:, span(j)])
+        value[j] = total.astype(BF16)
+        write[j].start()
+    for copy in write:
+        copy.wait()
 
 
 def combine_tail(table, rows, keep, received):
+    near = lambda v: pltpu.with_memory_space_constraint(v, pltpu.VMEM)
+    count, width = rows.shape
+    tokens = keep.shape[0]
+    block = width // CHUNKS
     return pl.pallas_call(
         combine_tail_body,
         out_shape=jax.ShapeDtypeStruct(keep.shape, BF16),
-        in_specs=[VMEM] * 4,
-        out_specs=VMEM,
+        in_specs=[VMEM, HBM, VMEM, VMEM],
+        out_specs=HBM,
+        scratch_shapes=[
+            pltpu.VMEM((CHUNKS, count, block), BF16),
+            pltpu.VMEM((CHUNKS, tokens, block), BF16),
+            pltpu.SemaphoreType.DMA((CHUNKS,)),
+            pltpu.SemaphoreType.DMA((CHUNKS,)),
+        ],
         compiler_params=pltpu.CompilerParams(vmem_limit_bytes=24 << 20),
         name="combine_tail",
-    )(*[pltpu.with_memory_space_constraint(v, pltpu.VMEM) for v in (table, rows, keep, received)])
+    )(near(table), rows, near(keep), near(received))
 
 
 def shared_apply(inputs, gate_matrix, up_matrix, down_matrix):

time: 183 us -> 184 us (level)
  no operation moved by 1% of the time
where the time goes in v3:
time: 184 us; the launch traced here: 183 us
  waiting for transfers between devices  87.4 us (48%)
  Pallas kernels  53.8 us (29%)
  starting transfers between devices  29.1 us (16%)
  matrix products  7.1 us (4%)
  other arithmetic  3.12 us (2%)
  local copies, waits for them, and re-layouts  2.47 us (1%)
    all_to_all x4, waiting for transfers between devices, exchange(): return lax.all_to_all(x, axis, split_axis=0, concat_axis=0, tiled=True)  82.4 us
    pallas_call x2, Pallas kernels, expert_apply(): pl.pallas_call(functools.partial(body, steps), out_shape=out, grid_spec=p...  34.8 us
    all_to_all x4, starting transfers between devices, exchange(): return lax.all_to_all(x, axis, split_axis=0, concat_axis=0, tiled=True)  28.2 us
    pallas_call x1, Pallas kernels, combine_head(): pl.pallas_call(combine_head_body, out_shape=(out, out), grid_spec=pltpu.P...  5.03 us
    pallas_call x1, Pallas kernels, dispatch_head(): pl.pallas_call(functools.partial(dispatch_head_body, experts), out_shape=...  4.52 us
    dot_general x1, matrix products, shared_apply(): return jnp.dot(hidden, down_matrix, preferred_element_type=F32)  4.42 us
  transfers between devices with their start and end apart: 10, of which 6 were waited for; matrix products, arithmetic and copies ran while one was open for 6% of the time, Pallas kernels for 25%

profile of v3, /device:TPU:0, one launch (start us, length us, event | category | flops | bytes accessed | tf_op | source)
XLA Modules:
  0.0 183.3 jit_solution(8252431677401724636)
XLA Ops:
  0.0 4.5 %dispatch_head.1 = bf16[512,3584]{1,0:T(8,128)(2,1)} custom-call(s32[1]{0:T(128)} %bitcast.core, s32[8,128]{1,0:T(8,128)} %bitcast.38, bf16[128,3584]{1,0:T(8,128)(2,1)} %tokens.3), custom_call_target="tpu_custom_call" | custom-call | tf_op jit(solution)/shard_map/dispatch_head/pallas_call | solution.py:107
  4.5 11.8 %all-to-all-start.2 = ((bf16[64,8,3584]{2,1,0:T(8,128)(2,1)}), bf16[64,8,3584]{2,1,0:T(8,128)(2,1)}, u32[]{:S(2)}, u32[]{:S(2)}) async-start(bf16[64,8,3584]{2,1,0:T(8,128)(2,1)} %bitcast.22), calls=%async_computation.2 | async-start | bytes 7340032 | tf_op jit(solution)/shard_map/all_to_all | solution.py:358
  16.3 0.1 collective-permute-start.1
  16.4 0.5 collective-permute-start.2
  16.9 0.1 collective-permute-start.3
  17.0 3.1 %dispatch_tail.1 = bf16[512,1792]{1,0:T(8,128)(2,1)} custom-call(s32[1]{0:T(128)} %bitcast.core, s32[8,128]{1,0:T(8,128)} %bitcast.39, bf16[128,3584]{1,0:T(8,128)(2,1)} %tokens.3), custom_call_target="tpu_custom_call" | custom-call | tf_op jit(solution)/shard_map/dispatch_tail/pallas_call | solution.py:133
  20.0 44.5 %all-to-all-done.2 = bf16[64,8,3584]{2,1,0:T(8,128)(2,1)} async-done(((bf16[64,8,3584]{2,1,0:T(8,128)(2,1)}), bf16[64,8,3584]{2,1,0:T(8,128)(2,1)}, u32[]{:S(2)}, u32[]{:S(2)}) %all-to-all-start.2) | async-done | bytes 3670048 | tf_op jit(solution)/shard_map/all_to_all | solution.py:358
  64.6 5.2 %all-to-all-start = ((bf16[64,8,1792]{2,1,0:T(8,128)(2,1)}), bf16[64,8,1792]{2,1,0:T(8,128)(2,1)S(1)}, u32[]{:S(2)}, u32[]{:S(2)}) async-start(bf16[64,8,1792]{2,1,0:T(8,128)(2,1)} %bitcast.25), calls=%async_computation | async-start | bytes 3670016 | tf_op jit(solution)/shard_map/all_to_all | solution.py:358
  69.7 0.0 collective-permute-done.1.g1
  69.8 0.0 collective-permute-done.3.d1
  69.8 20.3 %shard_map.92 = bf16[512,3584]{1,0:T(8,128)(2,1)} custom-call(s32[1]{0:T(128)} %bitcast.core, bf16[512,3584]{1,0:T(8,128)(2,1)} %bitcast.13.x, bf16[3584,512]{1,0:T(8,128)(2,1)} %bitcast.28, bf16[3584,512]{1,0:T(8,128)(2,1)} %bitcast.31, bf16[512,3584]{1,0:T(8,128)(2,1)} %bitcast.34, bf16[3584,512]{1,0:T(8,128)(2,1)} %collective-permute-done.1.g1, ...), custom_call_target="tpu_custom_call" | custom-call | flops 11274289152 | bytes 29360128 | tf_op jit(solution)/shard_map/pallas_call | solution.py:245
  90.1 6.4 %all-to-all-done = bf16[64,8,1792]{2,1,0:T(8,128)(2,1)S(1)} async-done(((bf16[64,8,1792]{2,1,0:T(8,128)(2,1)}), bf16[64,8,1792]{2,1,0:T(8,128)(2,1)S(1)}, u32[]{:S(2)}, u32[]{:S(2)}) %all-to-all-start) | async-done | bytes 1835040 | tf_op jit(solution)/shard_map/all_to_all | solution.py:358
  96.5 5.8 %all-to-all-start.3 = ((bf16[64,8,3584]{2,1,0:T(8,128)(2,1)}), bf16[64,8,3584]{2,1,0:T(8,128)(2,1)}, u32[]{:S(2)}, u32[]{:S(2)}) async-start(bf16[64,8,3584]{2,1,0:T(8,128)(2,1)} %bitcast.26), calls=%async_computation.3 | async-start | bytes 7340032 | tf_op jit(solution)/shard_map/all_to_all | solution.py:358
  102.3 0.1 dynamic-slice_bitcast_fusion
  102.4 0.1 collective-permute-start
  102.5 2.5 %collective-permute-done.x1 = bf16[256,1792]{1,0:T(8,128)(2,1)S(1)} collective-permute-done((bf16[256,1792]{1,0:T(8,128)(2,1)S(1)}, bf16[256,1792]{1,0:T(8,128)(2,1)S(1)}, u32[]{:S(2)}, u32[]{:S(2)}) %collective-permute-start) | collective-permute-done | bytes 917536 | tf_op jit(solution)/shard_map/ppermute | solution.py:382
  104.9 0.9 copy-done.4
  105.9 14.4 %shard_map.91 = (bf16[256,1792]{1,0:T(8,128)(2,1)}, bf16[256,1792]{1,0:T(8,128)(2,1)}) custom-call(s32[1]{0:T(128)} %bitcast.core, bf16[2,256,1792]{2,1,0:T(8,128)(2,1)} %bitcast.24, bf16[256,1792]{1,0:T(8,128)(2,1)} %copy-done.4, bf16[3584,512]{1,0:T(8,128)(2,1)} %bitcast.29, bf16[3584,512]{1,0:T(8,128)(2,1)} %bitcast.32, bf16[512,3584]{1,0:T(8,128)(2,1)} %bitcast.35, ...), custom_call_target="tpu_custom_call" | custom-call | flops 5637144576 | bytes 25690112 | tf_op jit(solution)/shard_map/pallas_call | solution.py:245
  120.3 0.1 collective-permute-start.4
  120.4 2.5 %collective-permute-done.4 = bf16[256,1792]{1,0:T(8,128)(2,1)S(1)} collective-permute-done((bf16[256,1792]{1,0:T(8,128)(2,1)}, bf16[256,1792]{1,0:T(8,128)(2,1)S(1)}, u32[]{:S(2)}, u32[]{:S(2)}) %collective-permute-start.4) | collective-permute-done | bytes 917536 | tf_op jit(solution)/shard_map/ppermute | solution.py:384
  123.0 3.1 %maximum_select_fusion = bf16[2,256,1792]{2,1,0:T(8,128)(2,1)} fusion(bf16[1,256,1792]{2,1,0:T(8,128)(2,1)S(1)} %bitcast.37, bf16[1,256,1792]{2,1,0:T(8,128)(2,1)} %bitcast.36, pred[]{:T(512)S(6)} %eq.3), kind=kLoop, calls=%fused_computation | loop fusion | flops 2752512 | bytes 3670017 | tf_op jit(solution)/shard_map/jit(_where)/select_n | solution.py:385
  126.1 21.9 %all-to-all-done.3 = bf16[64,8,3584]{2,1,0:T(8,128)(2,1)} async-done(((bf16[64,8,3584]{2,1,0:T(8,128)(2,1)}), bf16[64,8,3584]{2,1,0:T(8,128)(2,1)}, u32[]{:S(2)}, u32[]{:S(2)}) %all-to-all-start.3) | async-done | bytes 3670048 | tf_op jit(solution)/shard_map/all_to_all | solution.py:358
  148.0 5.5 %all-to-all-start.1 = ((bf16[64,8,1792]{2,1,0:T(8,128)(2,1)}), bf16[64,8,1792]{2,1,0:T(8,128)(2,1)}, u32[]{:S(2)}, u32[]{:S(2)}) async-start(bf16[64,8,1792]{2,1,0:T(8,128)(2,1)} %bitcast.10), calls=%async_computation.1 | async-start | bytes 3670016 | tf_op jit(solution)/shard_map/all_to_all | solution.py:358
  153.5 0.7 copy.10.ids
  154.3 0.7 copy.11.gates
  155.0 2.7 %weight_tables.1 = (bf16[256,512]{1,0:T(8,128)(2,1)}, bf16[256,512]{1,0:T(8,128)(2,1)}) custom-call(s32[1]{0:T(128)} %bitcast.core, s32[128,8]{1,0:T(8,128)} %copy.10.ids, f32[128,8]{1,0:T(8,128)} %copy.11.gates), custom_call_target="tpu_custom_call" | custom-call | tf_op jit(solution)/shard_map/weight_tables/pallas_call | solution.py:158
  157.7 2.7 %fusion.9 = f32[128,512]{1,0:T(8,128)S(1)} fusion(bf16[128,3584]{1,0:T(8,128)(2,1)S(1)} %copy-done.2, bf16[3584,512]{1,0:T(8,128)(2,1)} %param.15), kind=kOutput, calls=%fused_computation.12 | convolution fusion | flops 469762048 | bytes 4849664 | tf_op jit(solution)/shard_map/dot_general | solution.py:351
  160.4 0.0 copy-start.1
  160.4 4.4 %fusion.1.shared = f32[128,3584]{1,0:T(8,128)S(1)} fusion(bf16[512,3584]{1,0:T(8,128)(2,1)} %param.17, bf16[128,3584]{1,0:T(8,128)(2,1)S(1)} %copy-done.2, bf16[3584,512]{1,0:T(8,128)(2,1)} %param.16, f32[128,512]{1,0:T(8,128)S(1)} %fusion.9), kind=kOutput, calls=%fused_computation.3 | convolution fusion | flops 939917312 | bytes 10354688 | tf_op jit(solution)/shard_map/dot_general | solution.py:354
  164.8 5.0 %combine_head.1 = (f32[128,1792]{1,0:T(8,128)}, f32[128,1792]{1,0:T(8,128)S(1)}) custom-call(s32[1]{0:T(128)} %bitcast.core, bf16[256,512]{1,0:T(8,128)(2,1)S(1)} %copy-done.1, bf16[512,3584]{1,0:T(8,128)(2,1)} %bitcast.15.rows, f32[128,3584]{1,0:T(8,128)S(1)} %fusion.1.shared), custom_call_target="tpu_custom_call" | custom-call | tf_op jit(solution)/shard_map/combine_head/pallas_call | solution.py:288
  169.9 9.6 %all-to-all-done.1 = bf16[64,8,1792]{2,1,0:T(8,128)(2,1)} async-done(((bf16[64,8,1792]{2,1,0:T(8,128)(2,1)}), bf16[64,8,1792]{2,1,0:T(8,128)(2,1)}, u32[]{:S(2)}, u32[]{:S(2)}) %all-to-all-start.1) | async-done | bytes 1835040 | tf_op jit(solution)/shard_map/all_to_all | solution.py:358
  179.5 3.7 %combine_tail.1 = bf16[128,1792]{1,0:T(8,128)(2,1)} custom-call(bf16[256,512]{1,0:T(8,128)(2,1)S(1)} %copy-done, bf16[512,1792]{1,0:T(8,128)(2,1)} %bitcast.11.rows, f32[128,1792]{1,0:T(8,128)S(1)} %get-tuple-element.15.keep, f32[128,1792]{1,0:T(8,128)S(1)} %collective-permute-done.5.received), custom_call_target="tpu_custom_call" | custom-call | tf_op jit(solution)/shard_map/combine_tail/pallas_call | solution.py:334
  (15 shorter events, 0.0 us)
Async XLA Ops:
  4.5 60.0 %all-to-all-start.2 = ((bf16[64,8,3584]{2,1,0:T(8,128)(2,1)}), bf16[64,8,3584]{2,1,0:T(8,128)(2,1)}, u32[]{:S(2)}, u32[]{:S(2)}) async-start(bf16[64,8,3584]{2,1,0:T(8,128)(2,1)} %bitcast.22), calls=%async_computation.2 | async-start | bytes 7340032 | tf_op jit(solution)/shard_map/all_to_all | solution.py:358
  16.3 53.5 %collective-permute-start.1 = (bf16[3584,512]{1,0:T(8,128)(2,1)}, bf16[3584,512]{1,0:T(8,128)(2,1)}, u32[]{:S(2)}, u32[]{:S(2)}) collective-permute-start(bf16[3584,512]{1,0:T(8,128)(2,1)} %bitcast.27), channel_id=1, source_target_pairs={{0,1},{1,0},{2,3},{3,2},{4,5},{5,4},{6,7},{7,6},{8,9},{9,8},{10,11... | collective-permute-start | bytes 11010056 | tf_op jit(solution)/shard_map/ppermute | solution.py:370
  16.4 53.4 %collective-permute-start.2 = (bf16[3584,512]{1,0:T(8,128)(2,1)}, bf16[3584,512]{1,0:T(8,128)(2,1)}, u32[]{:S(2)}, u32[]{:S(2)}) collective-permute-start(bf16[3584,512]{1,0:T(8,128)(2,1)} %bitcast.30), channel_id=1, source_target_pairs={{0,1},{1,0},{2,3},{3,2},{4,5},{5,4},{6,7},{7,6},{8,9},{9,8},{10,11... | collective-permute-start | bytes 11010056 | tf_op jit(solution)/shard_map/ppermute | solution.py:370
  16.9 52.9 %collective-permute-start.3 = (bf16[512,3584]{1,0:T(8,128)(2,1)}, bf16[512,3584]{1,0:T(8,128)(2,1)}, u32[]{:S(2)}, u32[]{:S(2)}) collective-permute-start(bf16[512,3584]{1,0:T(8,128)(2,1)} %bitcast.33), channel_id=1, source_target_pairs={{0,1},{1,0},{2,3},{3,2},{4,5},{5,4},{6,7},{7,6},{8,9},{9,8},{10,11... | collective-permute-start | bytes 11010056 | tf_op jit(solution)/shard_map/ppermute | solution.py:370
  64.6 31.9 %all-to-all-start = ((bf16[64,8,1792]{2,1,0:T(8,128)(2,1)}), bf16[64,8,1792]{2,1,0:T(8,128)(2,1)S(1)}, u32[]{:S(2)}, u32[]{:S(2)}) async-start(bf16[64,8,1792]{2,1,0:T(8,128)(2,1)} %bitcast.25), calls=%async_computation | async-start | bytes 3670016 | tf_op jit(solution)/shard_map/all_to_all | solution.py:358
  96.5 5.8 %copy-start.3 = (bf16[64,8,1792]{2,1,0:T(8,128)(2,1)}, bf16[64,8,1792]{2,1,0:T(8,128)(2,1)S(1)}, u32[]{:S(2)}) copy-start(bf16[64,8,1792]{2,1,0:T(8,128)(2,1)S(1)} %all-to-all-done) | copy-start | bytes 5505028
  96.5 51.5 %all-to-all-start.3 = ((bf16[64,8,3584]{2,1,0:T(8,128)(2,1)}), bf16[64,8,3584]{2,1,0:T(8,128)(2,1)}, u32[]{:S(2)}, u32[]{:S(2)}) async-start(bf16[64,8,3584]{2,1,0:T(8,128)(2,1)} %bitcast.26), calls=%async_computation.3 | async-start | bytes 7340032 | tf_op jit(solution)/shard_map/all_to_all | solution.py:358
  102.4 2.6 %collective-permute-start = (bf16[256,1792]{1,0:T(8,128)(2,1)S(1)}, bf16[256,1792]{1,0:T(8,128)(2,1)S(1)}, u32[]{:S(2)}, u32[]{:S(2)}) collective-permute-start(bf16[256,1792]{1,0:T(8,128)(2,1)S(1)} %dynamic-slice_bitcast_fusion), channel_id=1, source_target_pairs={{0,1},{1,0},{2,3},{3,2},{4,5},{5,4},{6,7},{7,6},{8,9},{9,8},{10,11... | collective-permute-start | bytes 2752520 | tf_op jit(solution)/shard_map/ppermute | solution.py:382
  104.9 0.9 copy-start.4
  120.3 2.7 %collective-permute-start.4 = (bf16[256,1792]{1,0:T(8,128)(2,1)}, bf16[256,1792]{1,0:T(8,128)(2,1)S(1)}, u32[]{:S(2)}, u32[]{:S(2)}) collective-permute-start(bf16[256,1792]{1,0:T(8,128)(2,1)} %get-tuple-element.13), channel_id=1, source_target_pairs={{0,1},{1,0},{2,3},{3,2},{4,5},{5,4},{6,7},{7,6},{8,9},{9,8},{10,11... | collective-permute-start | bytes 2752520 | tf_op jit(solution)/shard_map/ppermute | solution.py:384
  123.0 30.5 %copy-start.5 = (s32[128,8]{0,1:T(8,128)S(1)}, s32[128,8]{0,1:T(8,128)}, u32[]{:S(2)}) copy-start(s32[128,8]{0,1:T(8,128)} %param.10) | copy-start | bytes 12292
  123.0 31.3 %copy-start.6 = (f32[128,8]{0,1:T(8,128)S(1)}, f32[128,8]{0,1:T(8,128)}, u32[]{:S(2)}) copy-start(f32[128,8]{0,1:T(8,128)} %param.11) | copy-start | bytes 12292
  123.0 34.7 %copy-start.2 = (bf16[128,3584]{1,0:T(8,128)(2,1)S(1)}, bf16[128,3584]{1,0:T(8,128)(2,1)}, u32[]{:S(2)}) copy-start(bf16[128,3584]{1,0:T(8,128)(2,1)} %tokens.3) | copy-start | bytes 2752516
  148.0 31.5 %all-to-all-start.1 = ((bf16[64,8,1792]{2,1,0:T(8,128)(2,1)}), bf16[64,8,1792]{2,1,0:T(8,128)(2,1)}, u32[]{:S(2)}, u32[]{:S(2)}) async-start(bf16[64,8,1792]{2,1,0:T(8,128)(2,1)} %bitcast.10), calls=%async_computation.1 | async-start | bytes 3670016 | tf_op jit(solution)/shard_map/all_to_all | solution.py:358
  160.4 4.5 %copy-start.1 = (bf16[256,512]{1,0:T(8,128)(2,1)S(1)}, bf16[256,512]{1,0:T(8,128)(2,1)}, u32[]{:S(2)}) copy-start(bf16[256,512]{1,0:T(8,128)(2,1)} %get-tuple-element.14.table) | copy-start | bytes 786436
  164.8 14.7 %copy-start = (bf16[256,512]{1,0:T(8,128)(2,1)S(1)}, bf16[256,512]{1,0:T(8,128)(2,1)}, u32[]{:S(2)}) copy-start(bf16[256,512]{1,0:T(8,128)(2,1)} %get-tuple-element.11.table) | copy-start | bytes 786436
  169.9 9.6 %collective-permute-start.5 = (f32[128,1792]{1,0:T(8,128)}, f32[128,1792]{1,0:T(8,128)S(1)}, u32[]{:S(2)}, u32[]{:S(2)}) collective-permute-start(f32[128,1792]{1,0:T(8,128)} %get-tuple-element.16), channel_id=1, source_target_pairs={{0,1},{1,0},{2,3},{3,2},{4,5},{5,4},{6,7},{7,6},{8,9},{9,8},{10,11... | collective-permute-start | bytes 2752520 | tf_op jit(solution)/shard_map/ppermute | solution.py:388
